TPU v7x, 32 devices: a whole 2x2x4 slice. The times are simulated.
32 devices in a mesh: groups: 2 (over x), feat: 16 (over z, y, core).
Axes of the slice: x: 2, y: 2, z: 4, core: 2. Of those that a mesh axis runs over, the one named last changes fastest.
Arguments:
- design: float32 [1024, 32768], P('groups', 'feat'), parts along dimension 0, may hold values from -6 to 6
- targets: float32 [1024, 128], P('groups'), parts along dimension 0, may hold values from -6 to 6
- coef_now: float32 [65536, 128], P(('groups', 'feat')), parts along dimension 0, may hold values from -1 to 1
- coef_prev: float32 [65536, 128], P(('groups', 'feat')), parts along dimension 0, may hold values from -1 to 1
- penalty: float32 [256], P('groups'), parts along dimension 0, may hold values from 0.1 to 1
- drop_mask: int32 [512], P(('groups', 'feat')), parts along dimension 0, may hold values from 0 to 1, as said below
- dest_shard: int32 [512], P(('groups', 'feat')), parts along dimension 0, may hold values from 0 to 15, as said below
Outputs:
- coef_out: float32 [98304, 128], P(('groups', 'feat')), parts along dimension 0
- design_out: float32 [1024, 49152], P('groups', 'feat'), parts along dimension 0
- duality_gap: float32 [256], P('groups'), parts along dimension 0
- dual_value: float32 [256], P('groups'), parts along dimension 0
- coef_l1: float32 [256], P('groups'), parts along dimension 0
There are 2 independent parts, one for each index of `groups`. A program takes and returns all parts, laid end to end along the dimension named above; each array names one. Nothing has to cross between parts.
Inputs may be any that keep to these rules, and one draw needn't show every extreme that they name: `drop_mask`: screening marks blocks to drop with 1; shards drop very different shares of their blocks. `dest_shard`: a block's destination is its own shard, except that any of the first 4 blocks of a shard may go to the shard before it (cyclically) and any of the last 4 blocks to the shard after it; no shard receives more than 24 surviving blocks, and some shard receives exactly 24 in every draw.
All inputs are finite; a program needn't handle non-finite values.
Results may differ from a plain program's by a relative error of at most 0.0003.
Values sent between devices are 32-bit elements; how exact they have to be, the bound alone decides.
No kernel may reach another device: no remote copies, remote signals or barrier semaphores. Data moves between devices by JAX's collectives and lax.ppermute only.
A program may use at most 64 MiB of HBM per device.

v0:
```python
import functools
import math

import jax
import jax.numpy as jnp
from jax import lax
from jax.experimental import pallas as pl
from jax.experimental.pallas import tpu as pltpu
from jax.sharding import PartitionSpec as P


START = 40
LANE = 128
AXIS = "feat"


def swap(value, bit):
    count = lax.axis_size(AXIS)
    return lax.ppermute(value, AXIS, [(i, i ^ bit) for i in range(count)])


def stages(count):
    return [1 << s for s in range(count.bit_length() - 1)]


def halves(values):
    high = values.astype(jnp.bfloat16)
    low = (values - high.astype(jnp.float32)).astype(jnp.bfloat16)
    return high, low


def mul(left, right):
    return lax.dot_general(left, right, (((1,), (0,)), ((), ())), preferred_element_type=jnp.float32)


def shrink(values, level):
    return values - jnp.clip(values, -level, level)


def forward(high, low, point):
    width = point.shape[1]
    ph, plo = halves(point)
    both = mul(high, jnp.concatenate([ph, plo], axis=1))
    return both[:, :width] + both[:, width:] + mul(low, ph)


def backward(high, low, turned):
    width = turned.shape[0] // 2
    both = mul(turned, high)
    return both[:width] + both[width:] + mul(turned[:width], low)


def hand_over(parity, total, keep_ref, send_ref):
    half = keep_ref.shape[0]
    keep_ref[...] = total[pl.ds(pl.multiple_of(parity * half, 8), half), :]
    send_ref[...] = total[pl.ds(pl.multiple_of((1 - parity) * half, 8), half), :]


def take_over(parity, own_ref, other_ref, targets_ref, whole):
    half = own_ref.shape[0]
    whole[pl.ds(pl.multiple_of(parity * half, 8), half), :] = own_ref[...]
    whole[pl.ds(pl.multiple_of((1 - parity) * half, 8), half), :] = other_ref[...]
    misfit = whole[...] - targets_ref[...]
    high, low = halves(misfit.T)
    return misfit, jnp.concatenate([high, low], axis=0)


def mask_of(drop_ref, dest_ref, start, count, shard):
    mask = jnp.int32(0)
    for k in range(count):
        moves = (drop_ref[start + k] == 0) & (dest_ref[start + k] == shard)
        mask = mask + jnp.where(moves, jnp.int32(1 << k), jnp.int32(0))
    return mask


def first_kernel(
    push, shards, chunk, me_ref, drop_ref, dest_ref, design_ref, now_ref, prev_ref,
    keep_ref, send_ref, near_ref, far_a_ref, far_b_ref, held_ref, high_ref, low_ref, base_ref, point_ref,
    prev, total, sems,
):
    me = me_ref[0]
    parity = me & 1
    rows, feats = design_ref.shape
    blocks = drop_ref.shape[0]
    edge = chunk // LANE
    steps = feats // chunk

    def copies(step):
        part = pl.ds(step * chunk, chunk)
        return [
            pltpu.make_async_copy(design_ref.at[:, part], held_ref.at[:, part], sems.at[0, step]),
            pltpu.make_async_copy(now_ref.at[part, :], base_ref.at[part, :], sems.at[1, step]),
            pltpu.make_async_copy(prev_ref.at[part, :], prev.at[part, :], sems.at[2, step]),
        ]

    for step in range(steps):
        for copy in copies(step):
            copy.start()
    for step in range(steps):
        for copy in copies(step):
            copy.wait()
        part = slice(step * chunk, (step + 1) * chunk)
        high, low = halves(held_ref[:, part])
        high_ref[:, part] = high
        low_ref[:, part] = low
        now = base_ref[part, :]
        point = now + push * (now - prev[part, :])
        point_ref[part, :] = point
        ahead = forward(high, low, point)
        if step == 0:
            total[...] = ahead
        else:
            total[...] += ahead
    hand_over(parity, total, keep_ref, send_ref)

    def put(right, near):
        block = held_ref[:, feats - chunk :] if right else held_ref[:, :chunk]
        if right:
            mask = mask_of(drop_ref, dest_ref, blocks - edge, edge, lax.rem(me + 1, shards))
        else:
            mask = mask_of(drop_ref, dest_ref, 0, edge, lax.rem(me + shards - 1, shards))
        ref = near_ref if near else far_a_ref
        if near:
            near_ref[:rows, :] = block
        else:
            far_a_ref[: rows // 2, :] = block[: rows // 2]
            far_b_ref[...] = block[rows // 2 :]
        ref[ref.shape[0] - 8 :, :] = jnp.full((8, chunk), mask.astype(jnp.float32), jnp.float32)

    @pl.when(parity == 1)
    def _():
        put(False, True)
        put(True, False)

    @pl.when(parity == 0)
    def _():
        put(True, True)
        put(False, False)


def descend_kernel(
    ahead, chunk, scale, level_scale, me_ref, high_ref, low_ref, point_ref, base_ref, own_ref, other_ref, targets_ref,
    penalty_ref, coef_ref, keep_ref, send_ref, *rest,
):
    total, split = rest[-2:]
    parity = me_ref[0] & 1
    _, feats = high_ref.shape
    width = targets_ref.shape[1]
    _, turned = take_over(parity, own_ref, other_ref, targets_ref, total)
    level = penalty_ref[...] * level_scale
    mass = jnp.zeros((1, width), jnp.float32)
    for step in range(feats // chunk):
        part = slice(step * chunk, (step + 1) * chunk)
        turn = backward(high_ref[:, part], low_ref[:, part], turned)
        coef = shrink(point_ref[part, :] - turn.T * (1.0 / scale), level)
        coef_ref[part, :] = coef
        if ahead is not None:
            coef = coef + ahead * (coef - base_ref[part, :])
            rest[0][part, :] = coef
        else:
            mass = mass + jnp.sum(jnp.abs(coef), axis=0, keepdims=True)
        ph, plo = halves(coef)
        split[part, :width] = ph
        split[part, width:] = plo
    both = mul(high_ref[...], split[...])
    total[...] = both[:, :width] + both[:, width:] + mul(low_ref[...], split[:, :width])
    hand_over(parity, total, keep_ref, send_ref)
    if ahead is None:
        mass_ref, near_ref, far_ref = rest[:3]
        mass_ref[...] = mass

        @pl.when(parity == 1)
        def _():
            near_ref[...] = coef_ref[: near_ref.shape[0], :]
            far_ref[...] = coef_ref[feats - far_ref.shape[0] :, :]

        @pl.when(parity == 0)
        def _():
            far_ref[...] = coef_ref[: far_ref.shape[0], :]
            near_ref[...] = coef_ref[feats - near_ref.shape[0] :, :]


def peak_kernel(
    chunk, me_ref, high_ref, low_ref, own_ref, other_ref, targets_ref, mass_ref, peak_ref, square_ref, cross_ref, total,
):
    parity = me_ref[0] & 1
    misfit, turned = take_over(parity, own_ref, other_ref, targets_ref, total)
    square_ref[...] = jnp.sum(misfit * misfit, axis=0, keepdims=True)
    cross_ref[...] = -jnp.sum(misfit * targets_ref[...], axis=0, keepdims=True)
    best = None
    for step in range(high_ref.shape[1] // chunk):
        part = slice(step * chunk, (step + 1) * chunk)
        turn = jnp.abs(backward(high_ref[:, part], low_ref[:, part], turned))
        for k in range(chunk // LANE):
            piece = turn[:, k * LANE : (k + 1) * LANE]
            best = piece if best is None else jnp.maximum(best, piece)
    half = peak_ref.shape[0] // 2
    peak_ref[:half] = jnp.broadcast_to(jnp.max(best.T, axis=0, keepdims=True), (half, LANE))
    peak_ref[half:] = jnp.broadcast_to(mass_ref[...], (half, LANE))


def cols(ref, index):
    return ref.at[:, pl.ds(pl.multiple_of(index * LANE, LANE), LANE)]


def cut(ref, first, count, index):
    return ref.at[first : first + count, pl.ds(pl.multiple_of(index * LANE, LANE), LANE)]


def sides(source, edge, blocks, parity):
    left = (source >= 0) & (source < edge)
    right = source >= edge + blocks
    inner = jnp.where(left, source, source - edge - blocks)
    near_side = (left & (parity == 1)) | (right & (parity == 0))
    far_side = (left & (parity == 0)) | (right & (parity == 1))
    return inner, near_side, far_side


def tabulate(me_ref, drop_ref, dest_ref, near_ref, far_ref, table_ref):
    blocks = drop_ref.shape[0]
    slots = table_ref.shape[0]
    edge = (slots - blocks) // 2
    me = me_ref[0]
    near = jnp.max(near_ref[near_ref.shape[0] - 8 :, :LANE]).astype(jnp.int32)
    far = jnp.max(far_ref[far_ref.shape[0] - 8 :, :LANE]).astype(jnp.int32)
    before = jnp.where((me & 1) == 1, near, far)
    after = jnp.where((me & 1) == 1, far, near)
    for slot in range(slots):
        table_ref[slot] = jnp.int32(-1)
    count = jnp.int32(0)
    for cand in range(slots):
        if cand < edge:
            here = (before >> cand) & 1
        elif cand < edge + blocks:
            k = cand - edge
            here = jnp.where((drop_ref[k] == 0) & (dest_ref[k] == me), jnp.int32(1), jnp.int32(0))
        else:
            here = (after >> (cand - edge - blocks)) & 1

        @pl.when(here == 1)
        def _(cand=cand, count=count):
            table_ref[count] = jnp.int32(cand)

        count = count + here


def place_own(first, last, edge, blocks, parity, table_ref, near_ref, own_ref, out_ref, blank, sems):
    rows = out_ref.shape[0]
    blank[...] = jnp.zeros_like(blank)
    for slot in range(first, last):
        source = table_ref[slot]
        inner, near_side, _ = sides(source, edge, blocks, parity)

        @pl.when(source < 0)
        def _(slot=slot):
            pltpu.make_async_copy(blank, cols(out_ref, slot), sems.at[slot]).start()

        @pl.when((source >= edge) & (source < edge + blocks))
        def _(slot=slot, source=source):
            pltpu.make_async_copy(cols(own_ref, source - edge), cols(out_ref, slot), sems.at[slot]).start()

        @pl.when(near_side)
        def _(slot=slot, inner=inner):
            pltpu.make_async_copy(cut(near_ref, 0, rows, inner), cols(out_ref, slot), sems.at[slot]).start()

    for slot in range(first, last):
        far_side = sides(table_ref[slot], edge, blocks, parity)[2]

        @pl.when(jnp.logical_not(far_side))
        def _(slot=slot):
            pltpu.make_async_copy(blank, cols(out_ref, slot), sems.at[slot]).wait()


def place_a_kernel(me_ref, drop_ref, dest_ref, near_ref, far_ref, own_ref, out_ref, table_ref, blank, sems):
    slots = table_ref.shape[0]
    blocks = drop_ref.shape[0]
    tabulate(me_ref, drop_ref, dest_ref, near_ref, far_ref, table_ref)
    place_own(0, slots // 2, (slots - blocks) // 2, blocks, me_ref[0] & 1, table_ref, near_ref, own_ref, out_ref, blank, sems)


def place_b_kernel(edge, me_ref, table_ref, near_ref, own_ref, given_ref, out_ref, blank, sems):
    slots = table_ref.shape[0]
    place_own(slots // 2, slots, edge, slots - 2 * edge, me_ref[0] & 1, table_ref, near_ref, own_ref, out_ref, blank, sems)


def place_c_kernel(edge, me_ref, table_ref, far_a_ref, far_b_ref, given_ref, out_ref, sems):
    slots = table_ref.shape[0]
    half = out_ref.shape[0] // 2
    parity = me_ref[0] & 1

    def each(slot, inner):
        return [
            pltpu.make_async_copy(cut(ref, 0, half, inner), cut(out_ref, k * half, half, slot), sems.at[k, slot])
            for k, ref in enumerate((far_a_ref, far_b_ref))
        ]

    for slot in range(slots):
        inner, _, far_side = sides(table_ref[slot], edge, slots - 2 * edge, parity)

        @pl.when(far_side)
        def _(slot=slot, inner=inner):
            for copy in each(slot, inner):
                copy.start()

    for slot in range(slots):
        far_side = sides(table_ref[slot], edge, slots - 2 * edge, parity)[2]

        @pl.when(far_side)
        def _(slot=slot):
            for copy in each(slot, 0):
                copy.wait()


def place_coef_kernel(edge, me_ref, table_ref, near_ref, own_ref, far_ref, out_ref, blank, sems):
    slots = table_ref.shape[0]
    own = slots - 2 * edge
    parity = me_ref[0] & 1
    blank[...] = jnp.zeros_like(blank)

    def rows(ref, index):
        return ref.at[pl.ds(pl.multiple_of(index * LANE, LANE), LANE), :]

    def copy(slot, src):
        return pltpu.make_async_copy(src, rows(out_ref, slot), sems.at[slot])

    for slot in range(slots):
        source = table_ref[slot]
        left = (source >= 0) & (source < edge)
        right = source >= edge + own
        inner = jnp.where(left, source, source - edge - own)

        @pl.when(source < 0)
        def _(slot=slot):
            copy(slot, blank).start()

        @pl.when((source >= edge) & (source < edge + own))
        def _(slot=slot, source=source):
            copy(slot, rows(own_ref, source - edge)).start()

        @pl.when((left & (parity == 1)) | (right & (parity == 0)))
        def _(slot=slot, inner=inner):
            copy(slot, rows(near_ref, inner)).start()

        @pl.when((left & (parity == 0)) | (right & (parity == 1)))
        def _(slot=slot, inner=inner):
            copy(slot, rows(far_ref, inner)).start()

    for slot in range(slots):
        copy(slot, blank).wait()


VM = pltpu.MemorySpace.VMEM
SM = pltpu.MemorySpace.SMEM


def whole():
    return pl.BlockSpec(memory_space=VM)


def scalars():
    return pl.BlockSpec(memory_space=SM)


def f32(*shape):
    return jax.ShapeDtypeStruct(shape, jnp.float32)


def body(design, targets, coef_now, coef_prev, penalty, drop_mask, dest_shard):
    samples, feats = design.shape
    width = targets.shape[1]
    shards = lax.axis_size(AXIS)
    me = lax.axis_index(AXIS).astype(jnp.int32).reshape(1)
    lipschitz = (math.sqrt(samples) + math.sqrt(feats * shards)) ** 2
    first_push = (START - 1) / (START + 2)
    second_push = START / (START + 3)
    blocks = feats // LANE
    edge = blocks // 4
    slots = blocks + 2 * edge
    chunk = edge * LANE
    steps = feats // chunk
    half = samples // 2
    bits = stages(shards)

    params = pltpu.CompilerParams(vmem_limit_bytes=24 << 20)
    line = penalty.reshape(1, width)
    anywhere = pl.BlockSpec(memory_space=pl.ANY)

    def in_hbm(value):
        return pltpu.with_memory_space_constraint(value, pltpu.MemorySpace.HBM)

    def b16(*shape):
        return jax.ShapeDtypeStruct(shape, jnp.bfloat16)

    drop, dest = in_hbm(drop_mask), in_hbm(dest_shard)
    keep, send, near, far_a, far_b, held, high, low, base, point = pl.pallas_call(
        functools.partial(first_kernel, first_push, shards, chunk),
        in_specs=[scalars()] * 3 + [anywhere] * 3,
        out_specs=[whole()] * 10,
        out_shape=[
            f32(half, width), f32(half, width), f32(samples + 8, chunk), f32(half + 8, chunk), f32(half, chunk),
            f32(samples, feats), b16(samples, feats), b16(samples, feats), f32(feats, width), f32(feats, width),
        ],
        scratch_shapes=[
            pltpu.VMEM((feats, width), jnp.float32),
            pltpu.VMEM((samples, width), jnp.float32),
            pltpu.SemaphoreType.DMA((3, steps)),
        ],
        compiler_params=params,
        name="first",
    )(me, drop, dest, in_hbm(design), in_hbm(coef_now), in_hbm(coef_prev))

    def inward(value):
        return swap(value, 1)

    def outward(value):
        pairs = [(i, (i + 1) % shards if i % 2 else (i - 1) % shards) for i in range(shards)]
        return lax.ppermute(value, AXIS, pairs)

    even_bits = bits[-1:] + bits[1:-1]
    odd_bits = bits[2:] + bits[1:2]

    def combine(keep, send):
        total = keep + swap(send, 1)
        for even, odd in zip(even_bits, odd_bits):
            pairs = [(i, i ^ (odd if i % 2 else even)) for i in range(shards)]
            total = total + lax.ppermute(total, AXIS, pairs)
        other = swap(total, 1)
        return total, other

    near_in = inward(near)
    far_a_in = outward(far_a)
    far_b_in = outward(far_b)

    sum_scratch = pltpu.VMEM((samples, width), jnp.float32)

    def descend(ahead, point, base, own, other):
        out_shape = [f32(feats, width), f32(half, width), f32(half, width)]
        if ahead is None:
            out_shape += [f32(1, width), f32(chunk, width), f32(chunk, width)]
        else:
            out_shape += [f32(feats, width)]
        return pl.pallas_call(
            functools.partial(descend_kernel, ahead, chunk, lipschitz, samples / lipschitz),
            in_specs=[scalars()] + [whole()] * 8,
            out_specs=[whole()] * len(out_shape),
            out_shape=out_shape,
            scratch_shapes=[sum_scratch, pltpu.VMEM((feats, 2 * width), jnp.bfloat16)],
            compiler_params=params,
            name="descend",
        )(me, high, low, point, base, own, other, targets, line)

    own, other = combine(keep, send)
    coef_one, keep, send, point = descend(second_push, point, base, own, other)
    own, other = combine(keep, send)
    coef_two, keep, send, mass, near, far = descend(None, point, coef_one, own, other)
    near_coef = inward(near)
    far_coef = outward(far)
    own, other = combine(keep, send)

    blank = pltpu.VMEM((samples, LANE), jnp.float32)
    out_form = f32(samples, slots * LANE)
    design_out, table = pl.pallas_call(
        place_a_kernel,
        in_specs=[scalars()] * 3 + [whole()] * 3,
        out_specs=[anywhere, scalars()],
        out_shape=[out_form, jax.ShapeDtypeStruct((slots,), jnp.int32)],
        scratch_shapes=[blank, pltpu.SemaphoreType.DMA((slots,))],
        compiler_params=params,
        name="place_a",
    )(me, drop, dest, near_in, far_a_in, held)
    design_out = pl.pallas_call(
        functools.partial(place_b_kernel, edge),
        in_specs=[scalars()] * 2 + [whole()] * 2 + [anywhere],
        out_specs=anywhere,
        out_shape=out_form,
        scratch_shapes=[blank, pltpu.SemaphoreType.DMA((slots,))],
        input_output_aliases={4: 0},
        compiler_params=params,
        name="place_b",
    )(me, table, near_in, held, design_out)
    design_out = pl.pallas_call(
        functools.partial(place_c_kernel, edge),
        in_specs=[scalars()] * 2 + [whole()] * 2 + [anywhere],
        out_specs=anywhere,
        out_shape=out_form,
        scratch_shapes=[pltpu.SemaphoreType.DMA((2, slots))],
        input_output_aliases={4: 0},
        compiler_params=params,
        name="place_c",
    )(me, table, far_a_in, far_b_in, design_out)

    tail, square, cross = pl.pallas_call(
        functools.partial(peak_kernel, chunk),
        in_specs=[scalars()] + [whole()] * 6,
        out_specs=[whole()] * 3,
        out_shape=[f32(16, width), f32(1, width), f32(1, width)],
        scratch_shapes=[sum_scratch],
        compiler_params=params,
        name="peak",
    )(me, high, low, own, other, targets, mass)
    is_peak = lax.broadcasted_iota(jnp.int32, (16, width), 0) < 8
    for bit in bits:
        got = swap(tail, bit)
        tail = jnp.where(is_peak, jnp.maximum(tail, got), tail + got)

    coef_out = pl.pallas_call(
        functools.partial(place_coef_kernel, edge),
        in_specs=[scalars(), scalars(), whole(), whole(), whole()],
        out_specs=anywhere,
        out_shape=f32(slots * LANE, width),
        scratch_shapes=[pltpu.VMEM((LANE, width), jnp.float32), pltpu.SemaphoreType.DMA((slots,))],
        compiler_params=params,
        name="place_coef",
    )(me, table, near_coef, coef_two, far_coef)

    peak, mass = tail[0], tail[8]
    dual_scale = jnp.maximum(penalty, peak / samples)
    ratio = penalty / dual_scale
    dual_value = (2.0 * ratio * cross[0] - ratio * ratio * square[0]) / (2.0 * samples)
    duality_gap = square[0] / (2.0 * samples) + penalty * mass - dual_value
    return (coef_out, design_out, duality_gap, dual_value, mass)


def solution(mesh):
    placed = (
        P("groups", "feat"),
        P("groups", None),
        P(("groups", "feat"), None),
        P(("groups", "feat"), None),
        P("groups"),
        P(("groups", "feat")),
        P(("groups", "feat")),
    )
    return jax.shard_map(
        body,
        mesh=mesh,
        in_specs=placed,
        out_specs=(
            P(("groups", "feat"), None),
            P("groups", "feat"),
            P("groups"),
            P("groups"),
            P("groups"),
        ),
        check_vma=False,
    )
```

profile of v0, /device:TPU:0, one launch (start us, length us, event | category | flops | bytes accessed | tf_op | source)
XLA Modules:
  0.0 112.4 jit_solution(3410402957261281515)
XLA Ops:
  0.7 4.4 %first.1 = (f32[256,128]{1,0:T(8,128)S(1)}, f32[256,128]{1,0:T(8,128)S(1)}, f32[520,512]{1,0:T(8,128)S(1)}, f32[264,512]{1,0:T(8,128)S(1)}, f32[256,512]{1,0:T(8...) custom-call(s32[1]{0:T(128)} %bitcast.me_ref, ...), custom_call_target="tpu_custom_call" | custom-call | tf_op jit(solution)/shard_map/first/pallas_call | solution.py:395
  6.5 4.0 %collective-permute-start.3 = (f32[256,128]{1,0:T(8,128)S(1)}, f32[256,128]{1,0:T(8,128)S(1)}, u32[]{:S(2)}, u32[]{:S(2)}) collective-permute-start(f32[256,128]{1,0:T(8,128)S(1)} %add.51), channel_id=1, source_target_pairs={{0,8},{1,5},{2,10},{3,7},{4,12},{5,1},{6,14},{7,3},{8,0},{9,13},{1... | collective-permute-start | bytes 393224 | tf_op jit(solution)/shard_map/ppermute | solution.py:426
  10.6 3.0 %collective-permute-done.3 = f32[256,128]{1,0:T(8,128)S(1)} collective-permute-done((f32[256,128]{1,0:T(8,128)S(1)}, f32[256,128]{1,0:T(8,128)S(1)}, u32[]{:S(2)}, u32[]{:S(2)}) %collective-permute-start.3) | collective-permute-done | bytes 131104 | tf_op jit(solution)/shard_map/ppermute | solution.py:426
  13.6 2.2 %collective-permute-start.4 = (f32[256,128]{1,0:T(8,128)S(1)}, f32[256,128]{1,0:T(8,128)S(1)}, u32[]{:S(2)}, u32[]{:S(2)}) collective-permute-start(f32[256,128]{1,0:T(8,128)S(1)} %add.52), channel_id=1, source_target_pairs={{0,2},{1,9},{2,0},{3,11},{4,6},{5,13},{6,4},{7,15},{8,10},{9,1},{1... | collective-permute-start | bytes 393224 | tf_op jit(solution)/shard_map/ppermute | solution.py:426
  15.8 2.9 %collective-permute-done.4 = f32[256,128]{1,0:T(8,128)S(1)} collective-permute-done((f32[256,128]{1,0:T(8,128)S(1)}, f32[256,128]{1,0:T(8,128)S(1)}, u32[]{:S(2)}, u32[]{:S(2)}) %collective-permute-start.4) | collective-permute-done | bytes 131104 | tf_op jit(solution)/shard_map/ppermute | solution.py:426
  18.8 2.5 %collective-permute-start.5 = (f32[256,128]{1,0:T(8,128)S(1)}, f32[256,128]{1,0:T(8,128)S(1)}, u32[]{:S(2)}, u32[]{:S(2)}) collective-permute-start(f32[256,128]{1,0:T(8,128)S(1)} %add.53), channel_id=1, source_target_pairs={{0,4},{1,3},{2,6},{3,1},{4,0},{5,7},{6,2},{7,5},{8,12},{9,11},{10,... | collective-permute-start | bytes 393224 | tf_op jit(solution)/shard_map/ppermute | solution.py:426
  21.3 2.9 %collective-permute-done.5 = f32[256,128]{1,0:T(8,128)S(1)} collective-permute-done((f32[256,128]{1,0:T(8,128)S(1)}, f32[256,128]{1,0:T(8,128)S(1)}, u32[]{:S(2)}, u32[]{:S(2)}) %collective-permute-start.5) | collective-permute-done | bytes 131104 | tf_op jit(solution)/shard_map/ppermute | solution.py:426
  25.7 2.4 %descend.2 = (f32[2048,128]{1,0:T(8,128)S(1)}, f32[256,128]{1,0:T(8,128)S(1)}, f32[256,128]{1,0:T(8,128)S(1)}, f32[2048,128]{1,0:T(8,128)S(1)}) custom-call(s32[1]{0:T(128)} %bitcast.me_ref, bf16[512,2048]{1,0:T(8,128)(2,1)S(1)} %get-tuple-element.34.high_ref, bf16[512,2048]{1,0:T(8,128)(2,1)S(1)} %get-tuple-element.35.low_ref, ...), custom_call_target="tpu_custom_call" | custom-call | tf_op jit(solution)/shard_map/descend/pallas_call | solution.py:442
  29.4 3.2 %collective-permute-start.8 = (f32[256,128]{1,0:T(8,128)S(1)}, f32[256,128]{1,0:T(8,128)S(1)}, u32[]{:S(2)}, u32[]{:S(2)}) collective-permute-start(f32[256,128]{1,0:T(8,128)S(1)} %add.55), channel_id=1, source_target_pairs={{0,8},{1,5},{2,10},{3,7},{4,12},{5,1},{6,14},{7,3},{8,0},{9,13},{1... | collective-permute-start | bytes 393224 | tf_op jit(solution)/shard_map/ppermute | solution.py:426
  32.7 2.9 %collective-permute-done.8 = f32[256,128]{1,0:T(8,128)S(1)} collective-permute-done((f32[256,128]{1,0:T(8,128)S(1)}, f32[256,128]{1,0:T(8,128)S(1)}, u32[]{:S(2)}, u32[]{:S(2)}) %collective-permute-start.8) | collective-permute-done | bytes 131104 | tf_op jit(solution)/shard_map/ppermute | solution.py:426
  37.2 3.4 %collective-permute-done.9 = f32[256,128]{1,0:T(8,128)S(1)} collective-permute-done((f32[256,128]{1,0:T(8,128)S(1)}, f32[256,128]{1,0:T(8,128)S(1)}, u32[]{:S(2)}, u32[]{:S(2)}) %collective-permute-start.9) | collective-permute-done | bytes 131104 | tf_op jit(solution)/shard_map/ppermute | solution.py:426
  40.7 3.0 %collective-permute-start.10 = (f32[256,128]{1,0:T(8,128)S(1)}, f32[256,128]{1,0:T(8,128)S(1)}, u32[]{:S(2)}, u32[]{:S(2)}) collective-permute-start(f32[256,128]{1,0:T(8,128)S(1)} %add.57), channel_id=1, source_target_pairs={{0,4},{1,3},{2,6},{3,1},{4,0},{5,7},{6,2},{7,5},{8,12},{9,11},{10,... | collective-permute-start | bytes 393224 | tf_op jit(solution)/shard_map/ppermute | solution.py:426
  43.7 2.9 %collective-permute-done.10 = f32[256,128]{1,0:T(8,128)S(1)} collective-permute-done((f32[256,128]{1,0:T(8,128)S(1)}, f32[256,128]{1,0:T(8,128)S(1)}, u32[]{:S(2)}, u32[]{:S(2)}) %collective-permute-start.10) | collective-permute-done | bytes 131104 | tf_op jit(solution)/shard_map/ppermute | solution.py:426
  48.0 2.4 %descend.3 = (f32[2048,128]{1,0:T(8,128)S(1)}, f32[256,128]{1,0:T(8,128)S(1)}, f32[256,128]{1,0:T(8,128)S(1)}, f32[1,128]{1,0:T(1,128)S(1)}, f32[512,128]{1,0:T(8,128)S(1)}, /*index=5*/f32[512,128]{1,0:T(8,128)S(1)}) custom-call(s32[1]{0:T(128)} %bitcast.me_ref, bf16[512,2048]{1,0:T(8,128)(2,1)S(1)} %get-tuple-element.34.high_ref, ...), custom_call_target="tpu_custom_call" | custom-call | tf_op jit(solution)/shard_map/descend/pallas_call | solution.py:442
  51.9 3.0 %collective-permute-start.16 = (f32[256,128]{1,0:T(8,128)S(1)}, f32[256,128]{1,0:T(8,128)S(1)}, u32[]{:S(2)}, u32[]{:S(2)}) collective-permute-start(f32[256,128]{1,0:T(8,128)S(1)} %add.59), channel_id=1, source_target_pairs={{0,8},{1,5},{2,10},{3,7},{4,12},{5,1},{6,14},{7,3},{8,0},{9,13},{1... | collective-permute-start | bytes 393224 | tf_op jit(solution)/shard_map/ppermute | solution.py:426
  54.9 3.0 %collective-permute-done.16 = f32[256,128]{1,0:T(8,128)S(1)} collective-permute-done((f32[256,128]{1,0:T(8,128)S(1)}, f32[256,128]{1,0:T(8,128)S(1)}, u32[]{:S(2)}, u32[]{:S(2)}) %collective-permute-start.16) | collective-permute-done | bytes 131104 | tf_op jit(solution)/shard_map/ppermute | solution.py:426
  59.4 3.4 %collective-permute-done.17 = f32[256,128]{1,0:T(8,128)S(1)} collective-permute-done((f32[256,128]{1,0:T(8,128)S(1)}, f32[256,128]{1,0:T(8,128)S(1)}, u32[]{:S(2)}, u32[]{:S(2)}) %collective-permute-start.17) | collective-permute-done | bytes 131104 | tf_op jit(solution)/shard_map/ppermute | solution.py:426
  62.9 2.9 %collective-permute-start.18 = (f32[256,128]{1,0:T(8,128)S(1)}, f32[256,128]{1,0:T(8,128)S(1)}, u32[]{:S(2)}, u32[]{:S(2)}) collective-permute-start(f32[256,128]{1,0:T(8,128)S(1)} %add.61), channel_id=1, source_target_pairs={{0,4},{1,3},{2,6},{3,1},{4,0},{5,7},{6,2},{7,5},{8,12},{9,11},{10,... | collective-permute-start | bytes 393224 | tf_op jit(solution)/shard_map/ppermute | solution.py:426
  65.8 2.9 %collective-permute-done.18 = f32[256,128]{1,0:T(8,128)S(1)} collective-permute-done((f32[256,128]{1,0:T(8,128)S(1)}, f32[256,128]{1,0:T(8,128)S(1)}, u32[]{:S(2)}, u32[]{:S(2)}) %collective-permute-start.18) | collective-permute-done | bytes 131104 | tf_op jit(solution)/shard_map/ppermute | solution.py:426
  68.9 5.4 %collective-permute-start.14 = (f32[256,512]{1,0:T(8,128)S(1)}, f32[256,512]{1,0:T(8,128)S(1)}, u32[]{:S(2)}, u32[]{:S(2)}) collective-permute-start(f32[256,512]{1,0:T(8,128)S(1)} %get-tuple-element.47), channel_id=1, source_target_pairs={{0,15},{1,2},{2,1},{3,4},{4,3},{5,6},{6,5},{7,8},{8,7},{9,10},{10,... | collective-permute-start | bytes 1572872 | tf_op jit(solution)/shard_map/ppermute | solution.py:417
  76.8 18.7 %collective-permute-done.21 = f32[16,128]{1,0:T(8,128)S(1)} collective-permute-done((f32[16,128]{1,0:T(8,128)S(1)}, f32[16,128]{1,0:T(8,128)S(1)}, u32[]{:S(2)}, u32[]{:S(2)}) %collective-permute-start.21) | collective-permute-done | bytes 8224 | tf_op jit(solution)/shard_map/ppermute | solution.py:19
  99.3 3.2 %collective-permute-start.13 = (f32[512,128]{1,0:T(8,128)S(1)}, f32[512,128]{1,0:T(8,128)S(1)}, u32[]{:S(2)}, u32[]{:S(2)}) collective-permute-start(f32[512,128]{1,0:T(8,128)S(1)} %get-tuple-element.46), channel_id=1, source_target_pairs={{0,15},{1,2},{2,1},{3,4},{4,3},{5,6},{6,5},{7,8},{8,7},{9,10},{10,... | collective-permute-start | bytes 786440 | tf_op jit(solution)/shard_map/ppermute | solution.py:417
  102.5 3.1 %place_a.1 = (f32[512,3072]{1,0:T(8,128)}, s32[24]{0:T(128)S(1)}) custom-call(s32[1]{0:T(128)} %bitcast.me_ref, s32[16]{0:T(128)} %drop_ref.3, s32[16]{0:T(128)} %dest_ref.3, f32[520,512]{1,0:T(8,128)S(1)} %collective-permute-done.near_ref, f32[264,512]{1,0:T(8,128)S(1)} %collective-permute-done.1.far_ref.far_a_ref, f32[512,2048]{1,0:T(8,128)S(1)} %get-tuple-element.32.own_ref), custom_call_target="tpu_custom_call" | custom-call | tf_op jit(solution)/shard_map/place_a/pallas_call | solution.py:462
  105.7 2.4 %place_b.1.given_ref = f32[512,3072]{1,0:T(8,128)} custom-call(s32[1]{0:T(128)} %bitcast.me_ref, s32[24]{0:T(128)S(1)} %get-tuple-element.33.table_ref, f32[520,512]{1,0:T(8,128)S(1)} %collective-permute-done.near_ref, f32[512,2048]{1,0:T(8,128)S(1)} %get-tuple-element.32.own_ref, ...), custom_call_target="tpu_custom_call", output_to_operand_aliasing={{}: (4, {})} | custom-call | tf_op jit(solution)/shard_map/place_b/pallas_call | solution.py:471
  (54 shorter events, 21.2 us)
Async XLA Ops:
  5.0 1.5 %collective-permute-start.2 = (f32[256,128]{1,0:T(8,128)S(1)}, f32[256,128]{1,0:T(8,128)S(1)}, u32[]{:S(2)}, u32[]{:S(2)}) collective-permute-start(f32[256,128]{1,0:T(8,128)S(1)} %get-tuple-element.39), channel_id=1, source_target_pairs={{0,1},{1,0},{2,3},{3,2},{4,5},{5,4},{6,7},{7,6},{8,9},{9,8},{10,11... | collective-permute-start | bytes 393224 | tf_op jit(solution)/shard_map/ppermute | solution.py:19
  6.5 7.0 %collective-permute-start.3 = (f32[256,128]{1,0:T(8,128)S(1)}, f32[256,128]{1,0:T(8,128)S(1)}, u32[]{:S(2)}, u32[]{:S(2)}) collective-permute-start(f32[256,128]{1,0:T(8,128)S(1)} %add.51), channel_id=1, source_target_pairs={{0,8},{1,5},{2,10},{3,7},{4,12},{5,1},{6,14},{7,3},{8,0},{9,13},{1... | collective-permute-start | bytes 393224 | tf_op jit(solution)/shard_map/ppermute | solution.py:426
  13.6 5.2 %collective-permute-start.4 = (f32[256,128]{1,0:T(8,128)S(1)}, f32[256,128]{1,0:T(8,128)S(1)}, u32[]{:S(2)}, u32[]{:S(2)}) collective-permute-start(f32[256,128]{1,0:T(8,128)S(1)} %add.52), channel_id=1, source_target_pairs={{0,2},{1,9},{2,0},{3,11},{4,6},{5,13},{6,4},{7,15},{8,10},{9,1},{1... | collective-permute-start | bytes 393224 | tf_op jit(solution)/shard_map/ppermute | solution.py:426
  18.8 5.4 %collective-permute-start.5 = (f32[256,128]{1,0:T(8,128)S(1)}, f32[256,128]{1,0:T(8,128)S(1)}, u32[]{:S(2)}, u32[]{:S(2)}) collective-permute-start(f32[256,128]{1,0:T(8,128)S(1)} %add.53), channel_id=1, source_target_pairs={{0,4},{1,3},{2,6},{3,1},{4,0},{5,7},{6,2},{7,5},{8,12},{9,11},{10,... | collective-permute-start | bytes 393224 | tf_op jit(solution)/shard_map/ppermute | solution.py:426
  24.2 1.4 %collective-permute-start.6 = (f32[256,128]{1,0:T(8,128)S(1)}, f32[256,128]{1,0:T(8,128)S(1)}, u32[]{:S(2)}, u32[]{:S(2)}) collective-permute-start(f32[256,128]{1,0:T(8,128)S(1)} %add.54.own_ref), channel_id=1, source_target_pairs={{0,1},{1,0},{2,3},{3,2},{4,5},{5,4},{6,7},{7,6},{8,9},{9,8},{10,11... | collective-permute-start | bytes 393224 | tf_op jit(solution)/shard_map/ppermute | solution.py:19
  28.0 1.4 %collective-permute-start.7 = (f32[256,128]{1,0:T(8,128)S(1)}, f32[256,128]{1,0:T(8,128)S(1)}, u32[]{:S(2)}, u32[]{:S(2)}) collective-permute-start(f32[256,128]{1,0:T(8,128)S(1)} %get-tuple-element.43), channel_id=1, source_target_pairs={{0,1},{1,0},{2,3},{3,2},{4,5},{5,4},{6,7},{7,6},{8,9},{9,8},{10,11... | collective-permute-start | bytes 393224 | tf_op jit(solution)/shard_map/ppermute | solution.py:19
  29.4 6.2 %collective-permute-start.8 = (f32[256,128]{1,0:T(8,128)S(1)}, f32[256,128]{1,0:T(8,128)S(1)}, u32[]{:S(2)}, u32[]{:S(2)}) collective-permute-start(f32[256,128]{1,0:T(8,128)S(1)} %add.55), channel_id=1, source_target_pairs={{0,8},{1,5},{2,10},{3,7},{4,12},{5,1},{6,14},{7,3},{8,0},{9,13},{1... | collective-permute-start | bytes 393224 | tf_op jit(solution)/shard_map/ppermute | solution.py:426
  35.7 5.0 %collective-permute-start.9 = (f32[256,128]{1,0:T(8,128)S(1)}, f32[256,128]{1,0:T(8,128)S(1)}, u32[]{:S(2)}, u32[]{:S(2)}) collective-permute-start(f32[256,128]{1,0:T(8,128)S(1)} %add.56), channel_id=1, source_target_pairs={{0,2},{1,9},{2,0},{3,11},{4,6},{5,13},{6,4},{7,15},{8,10},{9,1},{1... | collective-permute-start | bytes 393224 | tf_op jit(solution)/shard_map/ppermute | solution.py:426
  40.7 5.9 %collective-permute-start.10 = (f32[256,128]{1,0:T(8,128)S(1)}, f32[256,128]{1,0:T(8,128)S(1)}, u32[]{:S(2)}, u32[]{:S(2)}) collective-permute-start(f32[256,128]{1,0:T(8,128)S(1)} %add.57), channel_id=1, source_target_pairs={{0,4},{1,3},{2,6},{3,1},{4,0},{5,7},{6,2},{7,5},{8,12},{9,11},{10,... | collective-permute-start | bytes 393224 | tf_op jit(solution)/shard_map/ppermute | solution.py:426
  46.6 1.4 %collective-permute-start.11 = (f32[256,128]{1,0:T(8,128)S(1)}, f32[256,128]{1,0:T(8,128)S(1)}, u32[]{:S(2)}, u32[]{:S(2)}) collective-permute-start(f32[256,128]{1,0:T(8,128)S(1)} %add.58.own_ref), channel_id=1, source_target_pairs={{0,1},{1,0},{2,3},{3,2},{4,5},{5,4},{6,7},{7,6},{8,9},{9,8},{10,11... | collective-permute-start | bytes 393224 | tf_op jit(solution)/shard_map/ppermute | solution.py:19
  50.5 1.4 %collective-permute-start.15 = (f32[256,128]{1,0:T(8,128)S(1)}, f32[256,128]{1,0:T(8,128)S(1)}, u32[]{:S(2)}, u32[]{:S(2)}) collective-permute-start(f32[256,128]{1,0:T(8,128)S(1)} %get-tuple-element.50), channel_id=1, source_target_pairs={{0,1},{1,0},{2,3},{3,2},{4,5},{5,4},{6,7},{7,6},{8,9},{9,8},{10,11... | collective-permute-start | bytes 393224 | tf_op jit(solution)/shard_map/ppermute | solution.py:19
  51.9 5.9 %collective-permute-start.16 = (f32[256,128]{1,0:T(8,128)S(1)}, f32[256,128]{1,0:T(8,128)S(1)}, u32[]{:S(2)}, u32[]{:S(2)}) collective-permute-start(f32[256,128]{1,0:T(8,128)S(1)} %add.59), channel_id=1, source_target_pairs={{0,8},{1,5},{2,10},{3,7},{4,12},{5,1},{6,14},{7,3},{8,0},{9,13},{1... | collective-permute-start | bytes 393224 | tf_op jit(solution)/shard_map/ppermute | solution.py:426
  57.8 5.0 %collective-permute-start.17 = (f32[256,128]{1,0:T(8,128)S(1)}, f32[256,128]{1,0:T(8,128)S(1)}, u32[]{:S(2)}, u32[]{:S(2)}) collective-permute-start(f32[256,128]{1,0:T(8,128)S(1)} %add.60), channel_id=1, source_target_pairs={{0,2},{1,9},{2,0},{3,11},{4,6},{5,13},{6,4},{7,15},{8,10},{9,1},{1... | collective-permute-start | bytes 393224 | tf_op jit(solution)/shard_map/ppermute | solution.py:426
  62.9 5.9 %collective-permute-start.18 = (f32[256,128]{1,0:T(8,128)S(1)}, f32[256,128]{1,0:T(8,128)S(1)}, u32[]{:S(2)}, u32[]{:S(2)}) collective-permute-start(f32[256,128]{1,0:T(8,128)S(1)} %add.61), channel_id=1, source_target_pairs={{0,4},{1,3},{2,6},{3,1},{4,0},{5,7},{6,2},{7,5},{8,12},{9,11},{10,... | collective-permute-start | bytes 393224 | tf_op jit(solution)/shard_map/ppermute | solution.py:426
  65.8 36.7 %collective-permute-start = (f32[520,512]{1,0:T(8,128)S(1)}, f32[520,512]{1,0:T(8,128)S(1)}, u32[]{:S(2)}, u32[]{:S(2)}) collective-permute-start(f32[520,512]{1,0:T(8,128)S(1)} %get-tuple-element.30), channel_id=1, source_target_pairs={{0,1},{1,0},{2,3},{3,2},{4,5},{5,4},{6,7},{7,6},{8,9},{9,8},{10,11... | collective-permute-start | bytes 3194888 | tf_op jit(solution)/shard_map/ppermute | solution.py:19
  68.8 5.5 %collective-permute-start.19 = (f32[256,128]{1,0:T(8,128)S(1)}, f32[256,128]{1,0:T(8,128)S(1)}, u32[]{:S(2)}, u32[]{:S(2)}) collective-permute-start(f32[256,128]{1,0:T(8,128)S(1)} %add.62.own_ref), channel_id=1, source_target_pairs={{0,1},{1,0},{2,3},{3,2},{4,5},{5,4},{6,7},{7,6},{8,9},{9,8},{10,11... | collective-permute-start | bytes 393224 | tf_op jit(solution)/shard_map/ppermute | solution.py:19
  68.9 39.3 %collective-permute-start.14 = (f32[256,512]{1,0:T(8,128)S(1)}, f32[256,512]{1,0:T(8,128)S(1)}, u32[]{:S(2)}, u32[]{:S(2)}) collective-permute-start(f32[256,512]{1,0:T(8,128)S(1)} %get-tuple-element.47), channel_id=1, source_target_pairs={{0,15},{1,2},{2,1},{3,4},{4,3},{5,6},{6,5},{7,8},{8,7},{9,10},{10,... | collective-permute-start | bytes 1572872 | tf_op jit(solution)/shard_map/ppermute | solution.py:417
  74.3 28.2 %collective-permute-start.1 = (f32[264,512]{1,0:T(8,128)S(1)}, f32[264,512]{1,0:T(8,128)S(1)}, u32[]{:S(2)}, u32[]{:S(2)}) collective-permute-start(f32[264,512]{1,0:T(8,128)S(1)} %get-tuple-element.31), channel_id=1, source_target_pairs={{0,15},{1,2},{2,1},{3,4},{4,3},{5,6},{6,5},{7,8},{8,7},{9,10},{10,... | collective-permute-start | bytes 1622024 | tf_op jit(solution)/shard_map/ppermute | solution.py:417
  75.5 1.2 %collective-permute-start.20 = (f32[16,128]{1,0:T(8,128)S(1)}, f32[16,128]{1,0:T(8,128)S(1)}, u32[]{:S(2)}, u32[]{:S(2)}) collective-permute-start(f32[16,128]{1,0:T(8,128)S(1)} %get-tuple-element.53), channel_id=1, source_target_pairs={{0,1},{1,0},{2,3},{3,2},{4,5},{5,4},{6,7},{7,6},{8,9},{9,8},{10,11... | collective-permute-start | bytes 24584 | tf_op jit(solution)/shard_map/ppermute | solution.py:19
  76.8 18.7 %collective-permute-start.21 = (f32[16,128]{1,0:T(8,128)S(1)}, f32[16,128]{1,0:T(8,128)S(1)}, u32[]{:S(2)}, u32[]{:S(2)}) collective-permute-start(f32[16,128]{1,0:T(8,128)S(1)} %add_select_fusion.3), channel_id=1, source_target_pairs={{0,2},{1,3},{2,0},{3,1},{4,6},{5,7},{6,4},{7,5},{8,10},{9,11},{10,... | collective-permute-start | bytes 24584 | tf_op jit(solution)/shard_map/ppermute | solution.py:19
  95.6 3.7 %collective-permute-start.22 = (f32[16,128]{1,0:T(8,128)S(1)}, f32[16,128]{1,0:T(8,128)S(1)}, u32[]{:S(2)}, u32[]{:S(2)}) collective-permute-start(f32[16,128]{1,0:T(8,128)S(1)} %add_select_fusion.2), channel_id=1, source_target_pairs={{0,4},{1,5},{2,6},{3,7},{4,0},{5,1},{6,2},{7,3},{8,12},{9,13},{10,... | collective-permute-start | bytes 24584 | tf_op jit(solution)/shard_map/ppermute | solution.py:19
  97.6 12.3 %collective-permute-start.12 = (f32[512,128]{1,0:T(8,128)S(1)}, f32[512,128]{1,0:T(8,128)S(1)}, u32[]{:S(2)}, u32[]{:S(2)}) collective-permute-start(f32[512,128]{1,0:T(8,128)S(1)} %get-tuple-element.44), channel_id=1, source_target_pairs={{0,1},{1,0},{2,3},{3,2},{4,5},{5,4},{6,7},{7,6},{8,9},{9,8},{10,11... | collective-permute-start | bytes 786440 | tf_op jit(solution)/shard_map/ppermute | solution.py:19
  99.3 10.7 %collective-permute-start.13 = (f32[512,128]{1,0:T(8,128)S(1)}, f32[512,128]{1,0:T(8,128)S(1)}, u32[]{:S(2)}, u32[]{:S(2)}) collective-permute-start(f32[512,128]{1,0:T(8,128)S(1)} %get-tuple-element.46), channel_id=1, source_target_pairs={{0,15},{1,2},{2,1},{3,4},{4,3},{5,6},{6,5},{7,8},{8,7},{9,10},{10,... | collective-permute-start | bytes 786440 | tf_op jit(solution)/shard_map/ppermute | solution.py:417
  102.5 9.3 %collective-permute-start.23 = (f32[16,128]{1,0:T(8,128)S(1)}, f32[16,128]{1,0:T(8,128)S(1)}, u32[]{:S(2)}, u32[]{:S(2)}) collective-permute-start(f32[16,128]{1,0:T(8,128)S(1)} %add_select_fusion.1), channel_id=1, source_target_pairs={{0,8},{1,9},{2,10},{3,11},{4,12},{5,13},{6,14},{7,15},{8,0},{9,1},... | collective-permute-start | bytes 24584 | tf_op jit(solution)/shard_map/ppermute | solution.py:19
  (2 other events, 50.0 us)
where the time goes:
time: 113 us; the launch traced here: 112 us
  waiting for transfers between devices  55.2 us (49%)
  starting transfers between devices  35.9 us (32%)
  Pallas kernels  19.5 us (17%)
    ppermute x9, waiting for transfers between devices, combine(): total = total + lax.ppermute(total, AXIS, pairs)  27.6 us
    ppermute x12, waiting for transfers between devices, swap(): return lax.ppermute(value, AXIS, [(i, i ^ bit) for i in range(count)])  27.6 us
    ppermute x9, starting transfers between devices, combine(): total = total + lax.ppermute(total, AXIS, pairs)  24 us
    ppermute x3, starting transfers between devices, outward(): return lax.ppermute(value, AXIS, pairs)  8.64 us
    pallas_call x2, Pallas kernels, descend(): pl.pallas_call(functools.partial(descend_kernel, ahead, chunk, lipschitz,...  4.76 us
    pallas_call x1, Pallas kernels, body(): pl.pallas_call(functools.partial(first_kernel, first_push, shards, chunk)...  4.35 us
    ppermute x12, starting transfers between devices, swap(): return lax.ppermute(value, AXIS, [(i, i ^ bit) for i in range(count)])  3.26 us
    pallas_call x1, Pallas kernels, body(): pl.pallas_call(place_a_kernel, in_specs=[scalars()] * 3 + [whole()] * 3,...  3.15 us
  transfers between devices with their start and end apart: 24, of which 17 were waited for; matrix products, arithmetic and copies ran while one was open for 0% of the time, Pallas kernels for 9%

commit v1 on v0

--- a/solution.py
+++ b/solution.py
@@ -56,13 +56,25 @@
     send_ref[...] = total[pl.ds(pl.multiple_of((1 - parity) * half, 8), half), :]
 
 
-def take_over(parity, own_ref, other_ref, targets_ref, whole):
-    half = own_ref.shape[0]
-    whole[pl.ds(pl.multiple_of(parity * half, 8), half), :] = own_ref[...]
-    whole[pl.ds(pl.multiple_of((1 - parity) * half, 8), half), :] = other_ref[...]
-    misfit = whole[...] - targets_ref[...]
+def rows_of(side, half):
+    return pl.ds(pl.multiple_of(side * half, half), half)
+
+
+def turned_misfit(side, sum_ref, targets_ref):
+    half = sum_ref.shape[0]
+    wanted = targets_ref[rows_of(side, half), :]
+    misfit = sum_ref[...] - wanted
     high, low = halves(misfit.T)
-    return misfit, jnp.concatenate([high, low], axis=0)
+    return misfit, wanted, jnp.concatenate([high, low], axis=0)
+
+
+def half_kernel(chunk, me_ref, high_ref, low_ref, own_ref, targets_ref, turn_ref):
+    side = me_ref[0] & 1
+    _, _, turned = turned_misfit(side, own_ref, targets_ref)
+    rows = rows_of(side, own_ref.shape[0])
+    for step in range(high_ref.shape[1] // chunk):
+        part = slice(step * chunk, (step + 1) * chunk)
+        turn_ref[:, part] = backward(high_ref[rows, part], low_ref[rows, part], turned)
 
 
 def mask_of(drop_ref, dest_ref, start, count, shard):
@@ -139,19 +151,20 @@
 
 
 def descend_kernel(
-    ahead, chunk, scale, level_scale, me_ref, high_ref, low_ref, point_ref, base_ref, own_ref, other_ref, targets_ref,
+    ahead, chunk, scale, level_scale, me_ref, high_ref, low_ref, point_ref, base_ref, turn_ref, other_ref, targets_ref,
     penalty_ref, coef_ref, keep_ref, send_ref, *rest,
 ):
     total, split = rest[-2:]
     parity = me_ref[0] & 1
     _, feats = high_ref.shape
     width = targets_ref.shape[1]
-    _, turned = take_over(parity, own_ref, other_ref, targets_ref, total)
+    _, _, turned = turned_misfit(1 - parity, other_ref, targets_ref)
+    across = rows_of(1 - parity, other_ref.shape[0])
     level = penalty_ref[...] * level_scale
     mass = jnp.zeros((1, width), jnp.float32)
     for step in range(feats // chunk):
         part = slice(step * chunk, (step + 1) * chunk)
-        turn = backward(high_ref[:, part], low_ref[:, part], turned)
+        turn = turn_ref[:, part] + backward(high_ref[across, part], low_ref[across, part], turned)
         coef = shrink(point_ref[part, :] - turn.T * (1.0 / scale), level)
         coef_ref[part, :] = coef
         if ahead is not None:
@@ -181,16 +194,18 @@
 
 
 def peak_kernel(
-    chunk, me_ref, high_ref, low_ref, own_ref, other_ref, targets_ref, mass_ref, peak_ref, square_ref, cross_ref, total,
+    chunk, me_ref, high_ref, low_ref, turn_ref, own_ref, other_ref, targets_ref, mass_ref, peak_ref, square_ref, cross_ref,
 ):
     parity = me_ref[0] & 1
-    misfit, turned = take_over(parity, own_ref, other_ref, targets_ref, total)
-    square_ref[...] = jnp.sum(misfit * misfit, axis=0, keepdims=True)
-    cross_ref[...] = -jnp.sum(misfit * targets_ref[...], axis=0, keepdims=True)
+    mine, wanted, _ = turned_misfit(parity, own_ref, targets_ref)
+    theirs, needed, turned = turned_misfit(1 - parity, other_ref, targets_ref)
+    across = rows_of(1 - parity, other_ref.shape[0])
+    square_ref[...] = jnp.sum(mine * mine + theirs * theirs, axis=0, keepdims=True)
+    cross_ref[...] = -jnp.sum(mine * wanted + theirs * needed, axis=0, keepdims=True)
     best = None
     for step in range(high_ref.shape[1] // chunk):
         part = slice(step * chunk, (step + 1) * chunk)
-        turn = jnp.abs(backward(high_ref[:, part], low_ref[:, part], turned))
+        turn = jnp.abs(turn_ref[:, part] + backward(high_ref[across, part], low_ref[across, part], turned))
         for k in range(chunk // LANE):
             piece = turn[:, k * LANE : (k + 1) * LANE]
             best = piece if best is None else jnp.maximum(best, piece)
@@ -425,7 +440,15 @@
             pairs = [(i, i ^ (odd if i % 2 else even)) for i in range(shards)]
             total = total + lax.ppermute(total, AXIS, pairs)
         other = swap(total, 1)
-        return total, other
+        turn = pl.pallas_call(
+            functools.partial(half_kernel, chunk),
+            in_specs=[scalars()] + [whole()] * 4,
+            out_specs=whole(),
+            out_shape=f32(width, feats),
+            compiler_params=params,
+            name="half",
+        )(me, high, low, total, targets)
+        return total, other, turn
 
     near_in = inward(near)
     far_a_in = outward(far_a)
@@ -433,7 +456,7 @@
 
     sum_scratch = pltpu.VMEM((samples, width), jnp.float32)
 
-    def descend(ahead, point, base, own, other):
+    def descend(ahead, point, base, turn, other):
         out_shape = [f32(feats, width), f32(half, width), f32(half, width)]
         if ahead is None:
             out_shape += [f32(1, width), f32(chunk, width), f32(chunk, width)]
@@ -447,15 +470,15 @@
             scratch_shapes=[sum_scratch, pltpu.VMEM((feats, 2 * width), jnp.bfloat16)],
             compiler_params=params,
             name="descend",
-        )(me, high, low, point, base, own, other, targets, line)
-
-    own, other = combine(keep, send)
-    coef_one, keep, send, point = descend(second_push, point, base, own, other)
-    own, other = combine(keep, send)
-    coef_two, keep, send, mass, near, far = descend(None, point, coef_one, own, other)
+        )(me, high, low, point, base, turn, other, targets, line)
+
+    own, other, turn = combine(keep, send)
+    coef_one, keep, send, point = descend(second_push, point, base, turn, other)
+    own, other, turn = combine(keep, send)
+    coef_two, keep, send, mass, near, far = descend(None, point, coef_one, turn, other)
     near_coef = inward(near)
     far_coef = outward(far)
-    own, other = combine(keep, send)
+    own, other, turn = combine(keep, send)
 
     blank = pltpu.VMEM((samples, LANE), jnp.float32)
     out_form = f32(samples, slots * LANE)
@@ -491,13 +514,12 @@
 
     tail, square, cross = pl.pallas_call(
         functools.partial(peak_kernel, chunk),
-        in_specs=[scalars()] + [whole()] * 6,
+        in_specs=[scalars()] + [whole()] * 7,
         out_specs=[whole()] * 3,
         out_shape=[f32(16, width), f32(1, width), f32(1, width)],
-        scratch_shapes=[sum_scratch],
         compiler_params=params,
         name="peak",
-    )(me, high, low, own, other, targets, mass)
+    )(me, high, low, turn, own, other, targets, mass)
     is_peak = lax.broadcasted_iota(jnp.int32, (16, width), 0) < 8
     for bit in bits:
         got = swap(tail, bit)

time: 113 us -> 112 us (level)
  waiting for transfers between devices: 55.2 us -> 53.7 us
    pallas_call x0 -> x3, Pallas kernels: none -> 1.87 us  [combine(): pl.pallas_call(functools.partial(half_kernel, chunk), in_specs=[scalars()...]
    ppermute x12, waiting for transfers between devices: 27.6 us -> 26.1 us  [swap(): return lax.ppermute(value, AXIS, [(i, i ^ bit) for i in range(count)])]
  transfers between devices with their start and end apart: 24 -> 24, of which waited for: 17 -> 17; matrix products, arithmetic and copies ran while one was open for 0% -> 0% of each run, Pallas kernels for 9% -> 11%
where the time goes in v1:
time: 112 us
  waiting for transfers between devices  53.7 us (48%)
  starting transfers between devices  35.9 us (32%)
  Pallas kernels  20.2 us (18%)
    ppermute x9, waiting for transfers between devices, combine(): total = total + lax.ppermute(total, AXIS, pairs)  27.6 us
    ppermute x12, waiting for transfers between devices, swap(): return lax.ppermute(value, AXIS, [(i, i ^ bit) for i in range(count)])  26.1 us
    ppermute x9, starting transfers between devices, combine(): total = total + lax.ppermute(total, AXIS, pairs)  24 us
    ppermute x3, starting transfers between devices, outward(): return lax.ppermute(value, AXIS, pairs)  8.65 us
    pallas_call x1, Pallas kernels, body(): pl.pallas_call(functools.partial(first_kernel, first_push, shards, chunk)...  4.35 us
    pallas_call x2, Pallas kernels, descend(): pl.pallas_call(functools.partial(descend_kernel, ahead, chunk, lipschitz,...  4.07 us
    ppermute x12, starting transfers between devices, swap(): return lax.ppermute(value, AXIS, [(i, i ^ bit) for i in range(count)])  3.26 us
    pallas_call x1, Pallas kernels, body(): pl.pallas_call(place_a_kernel, in_specs=[scalars()] * 3 + [whole()] * 3,...  3.15 us
  transfers between devices with their start and end apart: 24, of which 17 were waited for; matrix products, arithmetic and copies ran while one was open for 0% of the time, Pallas kernels for 11%

profile of v1, /device:TPU:0, one launch (start us, length us, event | category | flops | bytes accessed | tf_op | source)
XLA Modules:
  0.0 111.8 jit_solution(12215439603972707173)
XLA Ops:
  0.6 4.4 %first.1 = (f32[256,128]{1,0:T(8,128)S(1)}, f32[256,128]{1,0:T(8,128)S(1)}, f32[520,512]{1,0:T(8,128)S(1)}, f32[264,512]{1,0:T(8,128)S(1)}, f32[256,512]{1,0:T(8...) custom-call(s32[1]{0:T(128)} %bitcast.me_ref, ...), custom_call_target="tpu_custom_call" | custom-call | tf_op jit(solution)/shard_map/first/pallas_call | solution.py:410
  6.5 4.0 %collective-permute-start.3 = (f32[256,128]{1,0:T(8,128)S(1)}, f32[256,128]{1,0:T(8,128)S(1)}, u32[]{:S(2)}, u32[]{:S(2)}) collective-permute-start(f32[256,128]{1,0:T(8,128)S(1)} %add.51), channel_id=1, source_target_pairs={{0,8},{1,5},{2,10},{3,7},{4,12},{5,1},{6,14},{7,3},{8,0},{9,13},{1... | collective-permute-start | bytes 393224 | tf_op jit(solution)/shard_map/ppermute | solution.py:441
  10.6 3.0 %collective-permute-done.3 = f32[256,128]{1,0:T(8,128)S(1)} collective-permute-done((f32[256,128]{1,0:T(8,128)S(1)}, f32[256,128]{1,0:T(8,128)S(1)}, u32[]{:S(2)}, u32[]{:S(2)}) %collective-permute-start.3) | collective-permute-done | bytes 131104 | tf_op jit(solution)/shard_map/ppermute | solution.py:441
  13.6 2.2 %collective-permute-start.4 = (f32[256,128]{1,0:T(8,128)S(1)}, f32[256,128]{1,0:T(8,128)S(1)}, u32[]{:S(2)}, u32[]{:S(2)}) collective-permute-start(f32[256,128]{1,0:T(8,128)S(1)} %add.52), channel_id=1, source_target_pairs={{0,2},{1,9},{2,0},{3,11},{4,6},{5,13},{6,4},{7,15},{8,10},{9,1},{1... | collective-permute-start | bytes 393224 | tf_op jit(solution)/shard_map/ppermute | solution.py:441
  15.9 2.9 %collective-permute-done.4 = f32[256,128]{1,0:T(8,128)S(1)} collective-permute-done((f32[256,128]{1,0:T(8,128)S(1)}, f32[256,128]{1,0:T(8,128)S(1)}, u32[]{:S(2)}, u32[]{:S(2)}) %collective-permute-start.4) | collective-permute-done | bytes 131104 | tf_op jit(solution)/shard_map/ppermute | solution.py:441
  18.8 2.4 %collective-permute-start.5 = (f32[256,128]{1,0:T(8,128)S(1)}, f32[256,128]{1,0:T(8,128)S(1)}, u32[]{:S(2)}, u32[]{:S(2)}) collective-permute-start(f32[256,128]{1,0:T(8,128)S(1)} %add.53), channel_id=1, source_target_pairs={{0,4},{1,3},{2,6},{3,1},{4,0},{5,7},{6,2},{7,5},{8,12},{9,11},{10,... | collective-permute-start | bytes 393224 | tf_op jit(solution)/shard_map/ppermute | solution.py:441
  21.3 2.9 %collective-permute-done.5 = f32[256,128]{1,0:T(8,128)S(1)} collective-permute-done((f32[256,128]{1,0:T(8,128)S(1)}, f32[256,128]{1,0:T(8,128)S(1)}, u32[]{:S(2)}, u32[]{:S(2)}) %collective-permute-start.5) | collective-permute-done | bytes 131104 | tf_op jit(solution)/shard_map/ppermute | solution.py:441
  29.1 3.2 %collective-permute-start.8 = (f32[256,128]{1,0:T(8,128)S(1)}, f32[256,128]{1,0:T(8,128)S(1)}, u32[]{:S(2)}, u32[]{:S(2)}) collective-permute-start(f32[256,128]{1,0:T(8,128)S(1)} %add.55), channel_id=1, source_target_pairs={{0,8},{1,5},{2,10},{3,7},{4,12},{5,1},{6,14},{7,3},{8,0},{9,13},{1... | collective-permute-start | bytes 393224 | tf_op jit(solution)/shard_map/ppermute | solution.py:441
  32.3 2.9 %collective-permute-done.8 = f32[256,128]{1,0:T(8,128)S(1)} collective-permute-done((f32[256,128]{1,0:T(8,128)S(1)}, f32[256,128]{1,0:T(8,128)S(1)}, u32[]{:S(2)}, u32[]{:S(2)}) %collective-permute-start.8) | collective-permute-done | bytes 131104 | tf_op jit(solution)/shard_map/ppermute | solution.py:441
  36.9 3.4 %collective-permute-done.9 = f32[256,128]{1,0:T(8,128)S(1)} collective-permute-done((f32[256,128]{1,0:T(8,128)S(1)}, f32[256,128]{1,0:T(8,128)S(1)}, u32[]{:S(2)}, u32[]{:S(2)}) %collective-permute-start.9) | collective-permute-done | bytes 131104 | tf_op jit(solution)/shard_map/ppermute | solution.py:441
  40.3 3.0 %collective-permute-start.10 = (f32[256,128]{1,0:T(8,128)S(1)}, f32[256,128]{1,0:T(8,128)S(1)}, u32[]{:S(2)}, u32[]{:S(2)}) collective-permute-start(f32[256,128]{1,0:T(8,128)S(1)} %add.57), channel_id=1, source_target_pairs={{0,4},{1,3},{2,6},{3,1},{4,0},{5,7},{6,2},{7,5},{8,12},{9,11},{10,... | collective-permute-start | bytes 393224 | tf_op jit(solution)/shard_map/ppermute | solution.py:441
  43.3 2.9 %collective-permute-done.10 = f32[256,128]{1,0:T(8,128)S(1)} collective-permute-done((f32[256,128]{1,0:T(8,128)S(1)}, f32[256,128]{1,0:T(8,128)S(1)}, u32[]{:S(2)}, u32[]{:S(2)}) %collective-permute-start.10) | collective-permute-done | bytes 131104 | tf_op jit(solution)/shard_map/ppermute | solution.py:441
  47.7 2.1 %descend.3 = (f32[2048,128]{1,0:T(8,128)S(1)}, f32[256,128]{1,0:T(8,128)S(1)}, f32[256,128]{1,0:T(8,128)S(1)}, f32[1,128]{1,0:T(1,128)S(1)}, f32[512,128]{1,0:T(8,128)S(1)}, /*index=5*/f32[512,128]{1,0:T(8,128)S(1)}) custom-call(s32[1]{0:T(128)} %bitcast.me_ref, bf16[512,2048]{1,0:T(8,128)(2,1)S(1)} %get-tuple-element.34.high_ref, ...), custom_call_target="tpu_custom_call" | custom-call | tf_op jit(solution)/shard_map/descend/pallas_call | solution.py:465
  51.2 3.0 %collective-permute-start.16 = (f32[256,128]{1,0:T(8,128)S(1)}, f32[256,128]{1,0:T(8,128)S(1)}, u32[]{:S(2)}, u32[]{:S(2)}) collective-permute-start(f32[256,128]{1,0:T(8,128)S(1)} %add.59), channel_id=1, source_target_pairs={{0,8},{1,5},{2,10},{3,7},{4,12},{5,1},{6,14},{7,3},{8,0},{9,13},{1... | collective-permute-start | bytes 393224 | tf_op jit(solution)/shard_map/ppermute | solution.py:441
  54.2 3.0 %collective-permute-done.16 = f32[256,128]{1,0:T(8,128)S(1)} collective-permute-done((f32[256,128]{1,0:T(8,128)S(1)}, f32[256,128]{1,0:T(8,128)S(1)}, u32[]{:S(2)}, u32[]{:S(2)}) %collective-permute-start.16) | collective-permute-done | bytes 131104 | tf_op jit(solution)/shard_map/ppermute | solution.py:441
  58.7 3.5 %collective-permute-done.17 = f32[256,128]{1,0:T(8,128)S(1)} collective-permute-done((f32[256,128]{1,0:T(8,128)S(1)}, f32[256,128]{1,0:T(8,128)S(1)}, u32[]{:S(2)}, u32[]{:S(2)}) %collective-permute-start.17) | collective-permute-done | bytes 131104 | tf_op jit(solution)/shard_map/ppermute | solution.py:441
  62.2 2.9 %collective-permute-start.18 = (f32[256,128]{1,0:T(8,128)S(1)}, f32[256,128]{1,0:T(8,128)S(1)}, u32[]{:S(2)}, u32[]{:S(2)}) collective-permute-start(f32[256,128]{1,0:T(8,128)S(1)} %add.61), channel_id=1, source_target_pairs={{0,4},{1,3},{2,6},{3,1},{4,0},{5,7},{6,2},{7,5},{8,12},{9,11},{10,... | collective-permute-start | bytes 393224 | tf_op jit(solution)/shard_map/ppermute | solution.py:441
  65.1 2.9 %collective-permute-done.18 = f32[256,128]{1,0:T(8,128)S(1)} collective-permute-done((f32[256,128]{1,0:T(8,128)S(1)}, f32[256,128]{1,0:T(8,128)S(1)}, u32[]{:S(2)}, u32[]{:S(2)}) %collective-permute-start.18) | collective-permute-done | bytes 131104 | tf_op jit(solution)/shard_map/ppermute | solution.py:441
  68.2 5.4 %collective-permute-start.14 = (f32[256,512]{1,0:T(8,128)S(1)}, f32[256,512]{1,0:T(8,128)S(1)}, u32[]{:S(2)}, u32[]{:S(2)}) collective-permute-start(f32[256,512]{1,0:T(8,128)S(1)} %get-tuple-element.47), channel_id=1, source_target_pairs={{0,15},{1,2},{2,1},{3,4},{4,3},{5,6},{6,5},{7,8},{8,7},{9,10},{10,... | collective-permute-start | bytes 1572872 | tf_op jit(solution)/shard_map/ppermute | solution.py:432
  76.3 18.5 %collective-permute-done.21 = f32[16,128]{1,0:T(8,128)S(1)} collective-permute-done((f32[16,128]{1,0:T(8,128)S(1)}, f32[16,128]{1,0:T(8,128)S(1)}, u32[]{:S(2)}, u32[]{:S(2)}) %collective-permute-start.21) | collective-permute-done | bytes 8224 | tf_op jit(solution)/shard_map/ppermute | solution.py:19
  94.9 2.0 %collective-permute-start.22 = (f32[16,128]{1,0:T(8,128)S(1)}, f32[16,128]{1,0:T(8,128)S(1)}, u32[]{:S(2)}, u32[]{:S(2)}) collective-permute-start(f32[16,128]{1,0:T(8,128)S(1)} %add_select_fusion.2), channel_id=1, source_target_pairs={{0,4},{1,5},{2,6},{3,7},{4,0},{5,1},{6,2},{7,3},{8,12},{9,13},{10,... | collective-permute-start | bytes 24584 | tf_op jit(solution)/shard_map/ppermute | solution.py:19
  98.6 3.2 %collective-permute-start.13 = (f32[512,128]{1,0:T(8,128)S(1)}, f32[512,128]{1,0:T(8,128)S(1)}, u32[]{:S(2)}, u32[]{:S(2)}) collective-permute-start(f32[512,128]{1,0:T(8,128)S(1)} %get-tuple-element.46), channel_id=1, source_target_pairs={{0,15},{1,2},{2,1},{3,4},{4,3},{5,6},{6,5},{7,8},{8,7},{9,10},{10,... | collective-permute-start | bytes 786440 | tf_op jit(solution)/shard_map/ppermute | solution.py:432
  101.9 3.1 %place_a.1 = (f32[512,3072]{1,0:T(8,128)}, s32[24]{0:T(128)S(1)}) custom-call(s32[1]{0:T(128)} %bitcast.me_ref, s32[16]{0:T(128)} %drop_ref.3, s32[16]{0:T(128)} %dest_ref.3, f32[520,512]{1,0:T(8,128)S(1)} %collective-permute-done.near_ref, f32[264,512]{1,0:T(8,128)S(1)} %collective-permute-done.1.far_ref.far_a_ref, f32[512,2048]{1,0:T(8,128)S(1)} %get-tuple-element.32.own_ref), custom_call_target="tpu_custom_call" | custom-call | tf_op jit(solution)/shard_map/place_a/pallas_call | solution.py:485
  105.0 2.4 %place_b.1.given_ref = f32[512,3072]{1,0:T(8,128)} custom-call(s32[1]{0:T(128)} %bitcast.me_ref, s32[24]{0:T(128)S(1)} %get-tuple-element.33.table_ref, f32[520,512]{1,0:T(8,128)S(1)} %collective-permute-done.near_ref, f32[512,2048]{1,0:T(8,128)S(1)} %get-tuple-element.32.own_ref, ...), custom_call_target="tpu_custom_call", output_to_operand_aliasing={{}: (4, {})} | custom-call | tf_op jit(solution)/shard_map/place_b/pallas_call | solution.py:494
  (57 shorter events, 21.3 us)
Async XLA Ops:
  5.0 1.5 %collective-permute-start.2 = (f32[256,128]{1,0:T(8,128)S(1)}, f32[256,128]{1,0:T(8,128)S(1)}, u32[]{:S(2)}, u32[]{:S(2)}) collective-permute-start(f32[256,128]{1,0:T(8,128)S(1)} %get-tuple-element.39), channel_id=1, source_target_pairs={{0,1},{1,0},{2,3},{3,2},{4,5},{5,4},{6,7},{7,6},{8,9},{9,8},{10,11... | collective-permute-start | bytes 393224 | tf_op jit(solution)/shard_map/ppermute | solution.py:19
  6.5 7.0 %collective-permute-start.3 = (f32[256,128]{1,0:T(8,128)S(1)}, f32[256,128]{1,0:T(8,128)S(1)}, u32[]{:S(2)}, u32[]{:S(2)}) collective-permute-start(f32[256,128]{1,0:T(8,128)S(1)} %add.51), channel_id=1, source_target_pairs={{0,8},{1,5},{2,10},{3,7},{4,12},{5,1},{6,14},{7,3},{8,0},{9,13},{1... | collective-permute-start | bytes 393224 | tf_op jit(solution)/shard_map/ppermute | solution.py:441
  13.6 5.2 %collective-permute-start.4 = (f32[256,128]{1,0:T(8,128)S(1)}, f32[256,128]{1,0:T(8,128)S(1)}, u32[]{:S(2)}, u32[]{:S(2)}) collective-permute-start(f32[256,128]{1,0:T(8,128)S(1)} %add.52), channel_id=1, source_target_pairs={{0,2},{1,9},{2,0},{3,11},{4,6},{5,13},{6,4},{7,15},{8,10},{9,1},{1... | collective-permute-start | bytes 393224 | tf_op jit(solution)/shard_map/ppermute | solution.py:441
  18.8 5.4 %collective-permute-start.5 = (f32[256,128]{1,0:T(8,128)S(1)}, f32[256,128]{1,0:T(8,128)S(1)}, u32[]{:S(2)}, u32[]{:S(2)}) collective-permute-start(f32[256,128]{1,0:T(8,128)S(1)} %add.53), channel_id=1, source_target_pairs={{0,4},{1,3},{2,6},{3,1},{4,0},{5,7},{6,2},{7,5},{8,12},{9,11},{10,... | collective-permute-start | bytes 393224 | tf_op jit(solution)/shard_map/ppermute | solution.py:441
  24.2 1.4 %collective-permute-start.6 = (f32[256,128]{1,0:T(8,128)S(1)}, f32[256,128]{1,0:T(8,128)S(1)}, u32[]{:S(2)}, u32[]{:S(2)}) collective-permute-start(f32[256,128]{1,0:T(8,128)S(1)} %add.54.own_ref), channel_id=1, source_target_pairs={{0,1},{1,0},{2,3},{3,2},{4,5},{5,4},{6,7},{7,6},{8,9},{9,8},{10,11... | collective-permute-start | bytes 393224 | tf_op jit(solution)/shard_map/ppermute | solution.py:19
  27.6 1.4 %collective-permute-start.7 = (f32[256,128]{1,0:T(8,128)S(1)}, f32[256,128]{1,0:T(8,128)S(1)}, u32[]{:S(2)}, u32[]{:S(2)}) collective-permute-start(f32[256,128]{1,0:T(8,128)S(1)} %get-tuple-element.43), channel_id=1, source_target_pairs={{0,1},{1,0},{2,3},{3,2},{4,5},{5,4},{6,7},{7,6},{8,9},{9,8},{10,11... | collective-permute-start | bytes 393224 | tf_op jit(solution)/shard_map/ppermute | solution.py:19
  29.1 6.2 %collective-permute-start.8 = (f32[256,128]{1,0:T(8,128)S(1)}, f32[256,128]{1,0:T(8,128)S(1)}, u32[]{:S(2)}, u32[]{:S(2)}) collective-permute-start(f32[256,128]{1,0:T(8,128)S(1)} %add.55), channel_id=1, source_target_pairs={{0,8},{1,5},{2,10},{3,7},{4,12},{5,1},{6,14},{7,3},{8,0},{9,13},{1... | collective-permute-start | bytes 393224 | tf_op jit(solution)/shard_map/ppermute | solution.py:441
  35.3 5.0 %collective-permute-start.9 = (f32[256,128]{1,0:T(8,128)S(1)}, f32[256,128]{1,0:T(8,128)S(1)}, u32[]{:S(2)}, u32[]{:S(2)}) collective-permute-start(f32[256,128]{1,0:T(8,128)S(1)} %add.56), channel_id=1, source_target_pairs={{0,2},{1,9},{2,0},{3,11},{4,6},{5,13},{6,4},{7,15},{8,10},{9,1},{1... | collective-permute-start | bytes 393224 | tf_op jit(solution)/shard_map/ppermute | solution.py:441
  40.3 5.9 %collective-permute-start.10 = (f32[256,128]{1,0:T(8,128)S(1)}, f32[256,128]{1,0:T(8,128)S(1)}, u32[]{:S(2)}, u32[]{:S(2)}) collective-permute-start(f32[256,128]{1,0:T(8,128)S(1)} %add.57), channel_id=1, source_target_pairs={{0,4},{1,3},{2,6},{3,1},{4,0},{5,7},{6,2},{7,5},{8,12},{9,11},{10,... | collective-permute-start | bytes 393224 | tf_op jit(solution)/shard_map/ppermute | solution.py:441
  46.3 1.4 %collective-permute-start.11 = (f32[256,128]{1,0:T(8,128)S(1)}, f32[256,128]{1,0:T(8,128)S(1)}, u32[]{:S(2)}, u32[]{:S(2)}) collective-permute-start(f32[256,128]{1,0:T(8,128)S(1)} %add.58.own_ref), channel_id=1, source_target_pairs={{0,1},{1,0},{2,3},{3,2},{4,5},{5,4},{6,7},{7,6},{8,9},{9,8},{10,11... | collective-permute-start | bytes 393224 | tf_op jit(solution)/shard_map/ppermute | solution.py:19
  49.8 1.4 %collective-permute-start.15 = (f32[256,128]{1,0:T(8,128)S(1)}, f32[256,128]{1,0:T(8,128)S(1)}, u32[]{:S(2)}, u32[]{:S(2)}) collective-permute-start(f32[256,128]{1,0:T(8,128)S(1)} %get-tuple-element.50), channel_id=1, source_target_pairs={{0,1},{1,0},{2,3},{3,2},{4,5},{5,4},{6,7},{7,6},{8,9},{9,8},{10,11... | collective-permute-start | bytes 393224 | tf_op jit(solution)/shard_map/ppermute | solution.py:19
  51.2 5.9 %collective-permute-start.16 = (f32[256,128]{1,0:T(8,128)S(1)}, f32[256,128]{1,0:T(8,128)S(1)}, u32[]{:S(2)}, u32[]{:S(2)}) collective-permute-start(f32[256,128]{1,0:T(8,128)S(1)} %add.59), channel_id=1, source_target_pairs={{0,8},{1,5},{2,10},{3,7},{4,12},{5,1},{6,14},{7,3},{8,0},{9,13},{1... | collective-permute-start | bytes 393224 | tf_op jit(solution)/shard_map/ppermute | solution.py:441
  57.2 5.0 %collective-permute-start.17 = (f32[256,128]{1,0:T(8,128)S(1)}, f32[256,128]{1,0:T(8,128)S(1)}, u32[]{:S(2)}, u32[]{:S(2)}) collective-permute-start(f32[256,128]{1,0:T(8,128)S(1)} %add.60), channel_id=1, source_target_pairs={{0,2},{1,9},{2,0},{3,11},{4,6},{5,13},{6,4},{7,15},{8,10},{9,1},{1... | collective-permute-start | bytes 393224 | tf_op jit(solution)/shard_map/ppermute | solution.py:441
  62.2 5.9 %collective-permute-start.18 = (f32[256,128]{1,0:T(8,128)S(1)}, f32[256,128]{1,0:T(8,128)S(1)}, u32[]{:S(2)}, u32[]{:S(2)}) collective-permute-start(f32[256,128]{1,0:T(8,128)S(1)} %add.61), channel_id=1, source_target_pairs={{0,4},{1,3},{2,6},{3,1},{4,0},{5,7},{6,2},{7,5},{8,12},{9,11},{10,... | collective-permute-start | bytes 393224 | tf_op jit(solution)/shard_map/ppermute | solution.py:441
  65.1 36.7 %collective-permute-start = (f32[520,512]{1,0:T(8,128)S(1)}, f32[520,512]{1,0:T(8,128)S(1)}, u32[]{:S(2)}, u32[]{:S(2)}) collective-permute-start(f32[520,512]{1,0:T(8,128)S(1)} %get-tuple-element.30), channel_id=1, source_target_pairs={{0,1},{1,0},{2,3},{3,2},{4,5},{5,4},{6,7},{7,6},{8,9},{9,8},{10,11... | collective-permute-start | bytes 3194888 | tf_op jit(solution)/shard_map/ppermute | solution.py:19
  68.1 6.2 %collective-permute-start.19 = (f32[256,128]{1,0:T(8,128)S(1)}, f32[256,128]{1,0:T(8,128)S(1)}, u32[]{:S(2)}, u32[]{:S(2)}) collective-permute-start(f32[256,128]{1,0:T(8,128)S(1)} %add.62.own_ref), channel_id=1, source_target_pairs={{0,1},{1,0},{2,3},{3,2},{4,5},{5,4},{6,7},{7,6},{8,9},{9,8},{10,11... | collective-permute-start | bytes 393224 | tf_op jit(solution)/shard_map/ppermute | solution.py:19
  68.2 39.3 %collective-permute-start.14 = (f32[256,512]{1,0:T(8,128)S(1)}, f32[256,512]{1,0:T(8,128)S(1)}, u32[]{:S(2)}, u32[]{:S(2)}) collective-permute-start(f32[256,512]{1,0:T(8,128)S(1)} %get-tuple-element.47), channel_id=1, source_target_pairs={{0,15},{1,2},{2,1},{3,4},{4,3},{5,6},{6,5},{7,8},{8,7},{9,10},{10,... | collective-permute-start | bytes 1572872 | tf_op jit(solution)/shard_map/ppermute | solution.py:432
  73.6 28.2 %collective-permute-start.1 = (f32[264,512]{1,0:T(8,128)S(1)}, f32[264,512]{1,0:T(8,128)S(1)}, u32[]{:S(2)}, u32[]{:S(2)}) collective-permute-start(f32[264,512]{1,0:T(8,128)S(1)} %get-tuple-element.31), channel_id=1, source_target_pairs={{0,15},{1,2},{2,1},{3,4},{4,3},{5,6},{6,5},{7,8},{8,7},{9,10},{10,... | collective-permute-start | bytes 1622024 | tf_op jit(solution)/shard_map/ppermute | solution.py:432
  75.0 1.2 %collective-permute-start.20 = (f32[16,128]{1,0:T(8,128)S(1)}, f32[16,128]{1,0:T(8,128)S(1)}, u32[]{:S(2)}, u32[]{:S(2)}) collective-permute-start(f32[16,128]{1,0:T(8,128)S(1)} %get-tuple-element.53), channel_id=1, source_target_pairs={{0,1},{1,0},{2,3},{3,2},{4,5},{5,4},{6,7},{7,6},{8,9},{9,8},{10,11... | collective-permute-start | bytes 24584 | tf_op jit(solution)/shard_map/ppermute | solution.py:19
  76.3 18.5 %collective-permute-start.21 = (f32[16,128]{1,0:T(8,128)S(1)}, f32[16,128]{1,0:T(8,128)S(1)}, u32[]{:S(2)}, u32[]{:S(2)}) collective-permute-start(f32[16,128]{1,0:T(8,128)S(1)} %add_select_fusion.3), channel_id=1, source_target_pairs={{0,2},{1,3},{2,0},{3,1},{4,6},{5,7},{6,4},{7,5},{8,10},{9,11},{10,... | collective-permute-start | bytes 24584 | tf_op jit(solution)/shard_map/ppermute | solution.py:19
  94.9 3.7 %collective-permute-start.22 = (f32[16,128]{1,0:T(8,128)S(1)}, f32[16,128]{1,0:T(8,128)S(1)}, u32[]{:S(2)}, u32[]{:S(2)}) collective-permute-start(f32[16,128]{1,0:T(8,128)S(1)} %add_select_fusion.2), channel_id=1, source_target_pairs={{0,4},{1,5},{2,6},{3,7},{4,0},{5,1},{6,2},{7,3},{8,12},{9,13},{10,... | collective-permute-start | bytes 24584 | tf_op jit(solution)/shard_map/ppermute | solution.py:19
  96.9 12.3 %collective-permute-start.12 = (f32[512,128]{1,0:T(8,128)S(1)}, f32[512,128]{1,0:T(8,128)S(1)}, u32[]{:S(2)}, u32[]{:S(2)}) collective-permute-start(f32[512,128]{1,0:T(8,128)S(1)} %get-tuple-element.44), channel_id=1, source_target_pairs={{0,1},{1,0},{2,3},{3,2},{4,5},{5,4},{6,7},{7,6},{8,9},{9,8},{10,11... | collective-permute-start | bytes 786440 | tf_op jit(solution)/shard_map/ppermute | solution.py:19
  98.6 10.7 %collective-permute-start.13 = (f32[512,128]{1,0:T(8,128)S(1)}, f32[512,128]{1,0:T(8,128)S(1)}, u32[]{:S(2)}, u32[]{:S(2)}) collective-permute-start(f32[512,128]{1,0:T(8,128)S(1)} %get-tuple-element.46), channel_id=1, source_target_pairs={{0,15},{1,2},{2,1},{3,4},{4,3},{5,6},{6,5},{7,8},{8,7},{9,10},{10,... | collective-permute-start | bytes 786440 | tf_op jit(solution)/shard_map/ppermute | solution.py:432
  101.8 9.3 %collective-permute-start.23 = (f32[16,128]{1,0:T(8,128)S(1)}, f32[16,128]{1,0:T(8,128)S(1)}, u32[]{:S(2)}, u32[]{:S(2)}) collective-permute-start(f32[16,128]{1,0:T(8,128)S(1)} %add_select_fusion.1), channel_id=1, source_target_pairs={{0,8},{1,9},{2,10},{3,11},{4,12},{5,13},{6,14},{7,15},{8,0},{9,1},... | collective-permute-start | bytes 24584 | tf_op jit(solution)/shard_map/ppermute | solution.py:19
  (2 other events, 44.3 us)

commit v2 on v1

--- a/solution.py
+++ b/solution.py
@@ -37,23 +37,20 @@
     return values - jnp.clip(values, -level, level)
 
 
-def forward(high, low, point):
-    width = point.shape[1]
-    ph, plo = halves(point)
-    both = mul(high, jnp.concatenate([ph, plo], axis=1))
-    return both[:, :width] + both[:, width:] + mul(low, ph)
+def split_of(point):
+    return jnp.concatenate(halves(point), axis=1)
+
+
+def forward(high, low, split):
+    width = split.shape[1] // 2
+    both = mul(high, split)
+    return both[:, :width] + both[:, width:] + mul(low, split[:, :width])
 
 
 def backward(high, low, turned):
     width = turned.shape[0] // 2
     both = mul(turned, high)
     return both[:width] + both[width:] + mul(turned[:width], low)
-
-
-def hand_over(parity, total, keep_ref, send_ref):
-    half = keep_ref.shape[0]
-    keep_ref[...] = total[pl.ds(pl.multiple_of(parity * half, 8), half), :]
-    send_ref[...] = total[pl.ds(pl.multiple_of((1 - parity) * half, 8), half), :]
 
 
 def rows_of(side, half):
@@ -66,6 +63,11 @@
     misfit = sum_ref[...] - wanted
     high, low = halves(misfit.T)
     return misfit, wanted, jnp.concatenate([high, low], axis=0)
+
+
+def keep_kernel(me_ref, high_ref, low_ref, split_ref, keep_ref):
+    rows = rows_of(me_ref[0] & 1, keep_ref.shape[0])
+    keep_ref[...] = forward(high_ref[rows, :], low_ref[rows, :], split_ref[...])
 
 
 def half_kernel(chunk, me_ref, high_ref, low_ref, own_ref, targets_ref, turn_ref):
@@ -87,8 +89,8 @@
 
 def first_kernel(
     push, shards, chunk, me_ref, drop_ref, dest_ref, design_ref, now_ref, prev_ref,
-    keep_ref, send_ref, near_ref, far_a_ref, far_b_ref, held_ref, high_ref, low_ref, base_ref, point_ref,
-    prev, total, sems,
+    send_ref, split_ref, near_ref, far_a_ref, far_b_ref, held_ref, high_ref, low_ref, base_ref, point_ref,
+    prev, sems,
 ):
     me = me_ref[0]
     parity = me & 1
@@ -96,6 +98,7 @@
     blocks = drop_ref.shape[0]
     edge = chunk // LANE
     steps = feats // chunk
+    across = rows_of(1 - parity, send_ref.shape[0])
 
     def copies(step):
         part = pl.ds(step * chunk, chunk)
@@ -118,12 +121,12 @@
         now = base_ref[part, :]
         point = now + push * (now - prev[part, :])
         point_ref[part, :] = point
-        ahead = forward(high, low, point)
+        split_ref[part, :] = split_of(point)
+        ahead = forward(high_ref[across, part], low_ref[across, part], split_ref[part, :])
         if step == 0:
-            total[...] = ahead
+            send_ref[...] = ahead
         else:
-            total[...] += ahead
-    hand_over(parity, total, keep_ref, send_ref)
+            send_ref[...] += ahead
 
     def put(right, near):
         block = held_ref[:, feats - chunk :] if right else held_ref[:, :chunk]
@@ -152,9 +155,8 @@
 
 def descend_kernel(
     ahead, chunk, scale, level_scale, me_ref, high_ref, low_ref, point_ref, base_ref, turn_ref, other_ref, targets_ref,
-    penalty_ref, coef_ref, keep_ref, send_ref, *rest,
+    penalty_ref, coef_ref, send_ref, split_ref, *rest,
 ):
-    total, split = rest[-2:]
     parity = me_ref[0] & 1
     _, feats = high_ref.shape
     width = targets_ref.shape[1]
@@ -172,12 +174,8 @@
             rest[0][part, :] = coef
         else:
             mass = mass + jnp.sum(jnp.abs(coef), axis=0, keepdims=True)
-        ph, plo = halves(coef)
-        split[part, :width] = ph
-        split[part, width:] = plo
-    both = mul(high_ref[...], split[...])
-    total[...] = both[:, :width] + both[:, width:] + mul(low_ref[...], split[:, :width])
-    hand_over(parity, total, keep_ref, send_ref)
+        split_ref[part, :] = split_of(coef)
+    send_ref[...] = forward(high_ref[across, :], low_ref[across, :], split_ref[...])
     if ahead is None:
         mass_ref, near_ref, far_ref = rest[:3]
         mass_ref[...] = mass
@@ -407,17 +405,16 @@
         return jax.ShapeDtypeStruct(shape, jnp.bfloat16)
 
     drop, dest = in_hbm(drop_mask), in_hbm(dest_shard)
-    keep, send, near, far_a, far_b, held, high, low, base, point = pl.pallas_call(
+    send, split, near, far_a, far_b, held, high, low, base, point = pl.pallas_call(
         functools.partial(first_kernel, first_push, shards, chunk),
         in_specs=[scalars()] * 3 + [anywhere] * 3,
         out_specs=[whole()] * 10,
         out_shape=[
-            f32(half, width), f32(half, width), f32(samples + 8, chunk), f32(half + 8, chunk), f32(half, chunk),
+            f32(half, width), b16(feats, 2 * width), f32(samples + 8, chunk), f32(half + 8, chunk), f32(half, chunk),
             f32(samples, feats), b16(samples, feats), b16(samples, feats), f32(feats, width), f32(feats, width),
         ],
         scratch_shapes=[
             pltpu.VMEM((feats, width), jnp.float32),
-            pltpu.VMEM((samples, width), jnp.float32),
             pltpu.SemaphoreType.DMA((3, steps)),
         ],
         compiler_params=params,
@@ -434,8 +431,17 @@
     even_bits = bits[-1:] + bits[1:-1]
     odd_bits = bits[2:] + bits[1:2]
 
-    def combine(keep, send):
-        total = keep + swap(send, 1)
+    def combine(split, send):
+        got = swap(send, 1)
+        keep = pl.pallas_call(
+            keep_kernel,
+            in_specs=[scalars()] + [whole()] * 3,
+            out_specs=whole(),
+            out_shape=f32(half, width),
+            compiler_params=params,
+            name="keep",
+        )(me, high, low, split)
+        total = keep + got
         for even, odd in zip(even_bits, odd_bits):
             pairs = [(i, i ^ (odd if i % 2 else even)) for i in range(shards)]
             total = total + lax.ppermute(total, AXIS, pairs)
@@ -454,10 +460,9 @@
     far_a_in = outward(far_a)
     far_b_in = outward(far_b)
 
-    sum_scratch = pltpu.VMEM((samples, width), jnp.float32)
 
     def descend(ahead, point, base, turn, other):
-        out_shape = [f32(feats, width), f32(half, width), f32(half, width)]
+        out_shape = [f32(feats, width), f32(half, width), b16(feats, 2 * width)]
         if ahead is None:
             out_shape += [f32(1, width), f32(chunk, width), f32(chunk, width)]
         else:
@@ -467,18 +472,17 @@
             in_specs=[scalars()] + [whole()] * 8,
             out_specs=[whole()] * len(out_shape),
             out_shape=out_shape,
-            scratch_shapes=[sum_scratch, pltpu.VMEM((feats, 2 * width), jnp.bfloat16)],
             compiler_params=params,
             name="descend",
         )(me, high, low, point, base, turn, other, targets, line)
 
-    own, other, turn = combine(keep, send)
-    coef_one, keep, send, point = descend(second_push, point, base, turn, other)
-    own, other, turn = combine(keep, send)
-    coef_two, keep, send, mass, near, far = descend(None, point, coef_one, turn, other)
+    own, other, turn = combine(split, send)
+    coef_one, send, split, point = descend(second_push, point, base, turn, other)
+    own, other, turn = combine(split, send)
+    coef_two, send, split, mass, near, far = descend(None, point, coef_one, turn, other)
     near_coef = inward(near)
     far_coef = outward(far)
-    own, other, turn = combine(keep, send)
+    own, other, turn = combine(split, send)
 
     blank = pltpu.VMEM((samples, LANE), jnp.float32)
     out_form = f32(samples, slots * LANE)

time: 112 us -> 111 us (level)
  waiting for transfers between devices: 53.7 us -> 51.5 us
    ppermute x12, waiting for transfers between devices: 26.1 us -> 23.9 us  [swap(): return lax.ppermute(value, AXIS, [(i, i ^ bit) for i in range(count)])]
    pallas_call x0 -> x3, Pallas kernels: none -> 2.14 us  [combine(): pl.pallas_call(keep_kernel, in_specs=[scalars()] + [whole()] * 3, out_spe...]
    pallas_call x2, Pallas kernels: 4.07 us -> 2.82 us  [descend(): pl.pallas_call(functools.partial(descend_kernel, ahead, chunk, lipschitz,...]
  transfers between devices with their start and end apart: 24 -> 24, of which waited for: 17 -> 17; matrix products, arithmetic and copies ran while one was open for 0% -> 0% of each run, Pallas kernels for 11% -> 13%
where the time goes in v2:
time: 111 us; the launch traced here: 110 us
  waiting for transfers between devices  51.5 us (46%)
  starting transfers between devices  35.9 us (32%)
  Pallas kernels  21 us (19%)
    ppermute x9, waiting for transfers between devices, combine(): total = total + lax.ppermute(total, AXIS, pairs)  27.6 us
    ppermute x9, starting transfers between devices, combine(): total = total + lax.ppermute(total, AXIS, pairs)  24.1 us
    ppermute x12, waiting for transfers between devices, swap(): return lax.ppermute(value, AXIS, [(i, i ^ bit) for i in range(count)])  23.9 us
    ppermute x3, starting transfers between devices, outward(): return lax.ppermute(value, AXIS, pairs)  8.65 us
    pallas_call x1, Pallas kernels, body(): pl.pallas_call(functools.partial(first_kernel, first_push, shards, chunk)...  4.25 us
    ppermute x12, starting transfers between devices, swap(): return lax.ppermute(value, AXIS, [(i, i ^ bit) for i in range(count)])  3.19 us
    pallas_call x1, Pallas kernels, body(): pl.pallas_call(place_a_kernel, in_specs=[scalars()] * 3 + [whole()] * 3,...  3.15 us
    pallas_call x2, Pallas kernels, descend(): pl.pallas_call(functools.partial(descend_kernel, ahead, chunk, lipschitz,...  2.82 us
  transfers between devices with their start and end apart: 24, of which 17 were waited for; matrix products, arithmetic and copies ran while one was open for 0% of the time, Pallas kernels for 13%

profile of v2, /device:TPU:0, one launch (start us, length us, event | category | flops | bytes accessed | tf_op | source)
XLA Modules:
  0.0 110.4 jit_solution(12313633322057749005)
XLA Ops:
  0.6 4.3 %first.1 = (f32[256,128]{1,0:T(8,128)S(1)}, bf16[2048,256]{1,0:T(8,128)(2,1)S(1)}, f32[520,512]{1,0:T(8,128)S(1)}, f32[264,512]{1,0:T(8,128)S(1)}, f32[256,512]{...) custom-call(s32[1]{0:T(128)} %bitcast.me_ref, ...), custom_call_target="tpu_custom_call" | custom-call | tf_op jit(solution)/shard_map/first/pallas_call | solution.py:408
  6.4 4.1 %collective-permute-start.3 = (f32[256,128]{1,0:T(8,128)S(1)}, f32[256,128]{1,0:T(8,128)S(1)}, u32[]{:S(2)}, u32[]{:S(2)}) collective-permute-start(f32[256,128]{1,0:T(8,128)S(1)} %add.51), channel_id=1, source_target_pairs={{0,8},{1,5},{2,10},{3,7},{4,12},{5,1},{6,14},{7,3},{8,0},{9,13},{1... | collective-permute-start | bytes 393224 | tf_op jit(solution)/shard_map/ppermute | solution.py:447
  10.5 3.0 %collective-permute-done.3 = f32[256,128]{1,0:T(8,128)S(1)} collective-permute-done((f32[256,128]{1,0:T(8,128)S(1)}, f32[256,128]{1,0:T(8,128)S(1)}, u32[]{:S(2)}, u32[]{:S(2)}) %collective-permute-start.3) | collective-permute-done | bytes 131104 | tf_op jit(solution)/shard_map/ppermute | solution.py:447
  13.5 2.2 %collective-permute-start.4 = (f32[256,128]{1,0:T(8,128)S(1)}, f32[256,128]{1,0:T(8,128)S(1)}, u32[]{:S(2)}, u32[]{:S(2)}) collective-permute-start(f32[256,128]{1,0:T(8,128)S(1)} %add.52), channel_id=1, source_target_pairs={{0,2},{1,9},{2,0},{3,11},{4,6},{5,13},{6,4},{7,15},{8,10},{9,1},{1... | collective-permute-start | bytes 393224 | tf_op jit(solution)/shard_map/ppermute | solution.py:447
  15.7 2.9 %collective-permute-done.4 = f32[256,128]{1,0:T(8,128)S(1)} collective-permute-done((f32[256,128]{1,0:T(8,128)S(1)}, f32[256,128]{1,0:T(8,128)S(1)}, u32[]{:S(2)}, u32[]{:S(2)}) %collective-permute-start.4) | collective-permute-done | bytes 131104 | tf_op jit(solution)/shard_map/ppermute | solution.py:447
  18.7 2.5 %collective-permute-start.5 = (f32[256,128]{1,0:T(8,128)S(1)}, f32[256,128]{1,0:T(8,128)S(1)}, u32[]{:S(2)}, u32[]{:S(2)}) collective-permute-start(f32[256,128]{1,0:T(8,128)S(1)} %add.53), channel_id=1, source_target_pairs={{0,4},{1,3},{2,6},{3,1},{4,0},{5,7},{6,2},{7,5},{8,12},{9,11},{10,... | collective-permute-start | bytes 393224 | tf_op jit(solution)/shard_map/ppermute | solution.py:447
  21.2 2.9 %collective-permute-done.5 = f32[256,128]{1,0:T(8,128)S(1)} collective-permute-done((f32[256,128]{1,0:T(8,128)S(1)}, f32[256,128]{1,0:T(8,128)S(1)}, u32[]{:S(2)}, u32[]{:S(2)}) %collective-permute-start.5) | collective-permute-done | bytes 131104 | tf_op jit(solution)/shard_map/ppermute | solution.py:447
  28.3 3.3 %collective-permute-start.8 = (f32[256,128]{1,0:T(8,128)S(1)}, f32[256,128]{1,0:T(8,128)S(1)}, u32[]{:S(2)}, u32[]{:S(2)}) collective-permute-start(f32[256,128]{1,0:T(8,128)S(1)} %add.55), channel_id=1, source_target_pairs={{0,8},{1,5},{2,10},{3,7},{4,12},{5,1},{6,14},{7,3},{8,0},{9,13},{1... | collective-permute-start | bytes 393224 | tf_op jit(solution)/shard_map/ppermute | solution.py:447
  31.6 2.9 %collective-permute-done.8 = f32[256,128]{1,0:T(8,128)S(1)} collective-permute-done((f32[256,128]{1,0:T(8,128)S(1)}, f32[256,128]{1,0:T(8,128)S(1)}, u32[]{:S(2)}, u32[]{:S(2)}) %collective-permute-start.8) | collective-permute-done | bytes 131104 | tf_op jit(solution)/shard_map/ppermute | solution.py:447
  36.1 3.4 %collective-permute-done.9 = f32[256,128]{1,0:T(8,128)S(1)} collective-permute-done((f32[256,128]{1,0:T(8,128)S(1)}, f32[256,128]{1,0:T(8,128)S(1)}, u32[]{:S(2)}, u32[]{:S(2)}) %collective-permute-start.9) | collective-permute-done | bytes 131104 | tf_op jit(solution)/shard_map/ppermute | solution.py:447
  39.6 2.9 %collective-permute-start.10 = (f32[256,128]{1,0:T(8,128)S(1)}, f32[256,128]{1,0:T(8,128)S(1)}, u32[]{:S(2)}, u32[]{:S(2)}) collective-permute-start(f32[256,128]{1,0:T(8,128)S(1)} %add.57), channel_id=1, source_target_pairs={{0,4},{1,3},{2,6},{3,1},{4,0},{5,7},{6,2},{7,5},{8,12},{9,11},{10,... | collective-permute-start | bytes 393224 | tf_op jit(solution)/shard_map/ppermute | solution.py:447
  42.6 2.9 %collective-permute-done.10 = f32[256,128]{1,0:T(8,128)S(1)} collective-permute-done((f32[256,128]{1,0:T(8,128)S(1)}, f32[256,128]{1,0:T(8,128)S(1)}, u32[]{:S(2)}, u32[]{:S(2)}) %collective-permute-start.10) | collective-permute-done | bytes 131104 | tf_op jit(solution)/shard_map/ppermute | solution.py:447
  49.8 3.0 %collective-permute-start.16 = (f32[256,128]{1,0:T(8,128)S(1)}, f32[256,128]{1,0:T(8,128)S(1)}, u32[]{:S(2)}, u32[]{:S(2)}) collective-permute-start(f32[256,128]{1,0:T(8,128)S(1)} %add.59), channel_id=1, source_target_pairs={{0,8},{1,5},{2,10},{3,7},{4,12},{5,1},{6,14},{7,3},{8,0},{9,13},{1... | collective-permute-start | bytes 393224 | tf_op jit(solution)/shard_map/ppermute | solution.py:447
  52.8 3.0 %collective-permute-done.16 = f32[256,128]{1,0:T(8,128)S(1)} collective-permute-done((f32[256,128]{1,0:T(8,128)S(1)}, f32[256,128]{1,0:T(8,128)S(1)}, u32[]{:S(2)}, u32[]{:S(2)}) %collective-permute-start.16) | collective-permute-done | bytes 131104 | tf_op jit(solution)/shard_map/ppermute | solution.py:447
  57.4 3.4 %collective-permute-done.17 = f32[256,128]{1,0:T(8,128)S(1)} collective-permute-done((f32[256,128]{1,0:T(8,128)S(1)}, f32[256,128]{1,0:T(8,128)S(1)}, u32[]{:S(2)}, u32[]{:S(2)}) %collective-permute-start.17) | collective-permute-done | bytes 131104 | tf_op jit(solution)/shard_map/ppermute | solution.py:447
  60.8 2.9 %collective-permute-start.18 = (f32[256,128]{1,0:T(8,128)S(1)}, f32[256,128]{1,0:T(8,128)S(1)}, u32[]{:S(2)}, u32[]{:S(2)}) collective-permute-start(f32[256,128]{1,0:T(8,128)S(1)} %add.61), channel_id=1, source_target_pairs={{0,4},{1,3},{2,6},{3,1},{4,0},{5,7},{6,2},{7,5},{8,12},{9,11},{10,... | collective-permute-start | bytes 393224 | tf_op jit(solution)/shard_map/ppermute | solution.py:447
  63.8 2.9 %collective-permute-done.18 = f32[256,128]{1,0:T(8,128)S(1)} collective-permute-done((f32[256,128]{1,0:T(8,128)S(1)}, f32[256,128]{1,0:T(8,128)S(1)}, u32[]{:S(2)}, u32[]{:S(2)}) %collective-permute-start.18) | collective-permute-done | bytes 131104 | tf_op jit(solution)/shard_map/ppermute | solution.py:447
  66.8 5.4 %collective-permute-start.14 = (f32[256,512]{1,0:T(8,128)S(1)}, f32[256,512]{1,0:T(8,128)S(1)}, u32[]{:S(2)}, u32[]{:S(2)}) collective-permute-start(f32[256,512]{1,0:T(8,128)S(1)} %get-tuple-element.47), channel_id=1, source_target_pairs={{0,15},{1,2},{2,1},{3,4},{4,3},{5,6},{6,5},{7,8},{8,7},{9,10},{10,... | collective-permute-start | bytes 1572872 | tf_op jit(solution)/shard_map/ppermute | solution.py:429
  75.0 18.5 %collective-permute-done.21 = f32[16,128]{1,0:T(8,128)S(1)} collective-permute-done((f32[16,128]{1,0:T(8,128)S(1)}, f32[16,128]{1,0:T(8,128)S(1)}, u32[]{:S(2)}, u32[]{:S(2)}) %collective-permute-start.21) | collective-permute-done | bytes 8224 | tf_op jit(solution)/shard_map/ppermute | solution.py:19
  93.6 2.0 %collective-permute-start.22 = (f32[16,128]{1,0:T(8,128)S(1)}, f32[16,128]{1,0:T(8,128)S(1)}, u32[]{:S(2)}, u32[]{:S(2)}) collective-permute-start(f32[16,128]{1,0:T(8,128)S(1)} %add_select_fusion.2), channel_id=1, source_target_pairs={{0,4},{1,5},{2,6},{3,7},{4,0},{5,1},{6,2},{7,3},{8,12},{9,13},{10,... | collective-permute-start | bytes 24584 | tf_op jit(solution)/shard_map/ppermute | solution.py:19
  97.2 3.2 %collective-permute-start.13 = (f32[512,128]{1,0:T(8,128)S(1)}, f32[512,128]{1,0:T(8,128)S(1)}, u32[]{:S(2)}, u32[]{:S(2)}) collective-permute-start(f32[512,128]{1,0:T(8,128)S(1)} %get-tuple-element.46), channel_id=1, source_target_pairs={{0,15},{1,2},{2,1},{3,4},{4,3},{5,6},{6,5},{7,8},{8,7},{9,10},{10,... | collective-permute-start | bytes 786440 | tf_op jit(solution)/shard_map/ppermute | solution.py:429
  100.5 3.1 %place_a.1 = (f32[512,3072]{1,0:T(8,128)}, s32[24]{0:T(128)S(1)}) custom-call(s32[1]{0:T(128)} %bitcast.me_ref, s32[16]{0:T(128)} %drop_ref.3, s32[16]{0:T(128)} %dest_ref.3, f32[520,512]{1,0:T(8,128)S(1)} %collective-permute-done.near_ref, f32[264,512]{1,0:T(8,128)S(1)} %collective-permute-done.1.far_ref.far_a_ref, f32[512,2048]{1,0:T(8,128)S(1)} %get-tuple-element.32.own_ref), custom_call_target="tpu_custom_call" | custom-call | tf_op jit(solution)/shard_map/place_a/pallas_call | solution.py:489
  103.7 2.4 %place_b.1.given_ref = f32[512,3072]{1,0:T(8,128)} custom-call(s32[1]{0:T(128)} %bitcast.me_ref, s32[24]{0:T(128)S(1)} %get-tuple-element.33.table_ref, f32[520,512]{1,0:T(8,128)S(1)} %collective-permute-done.near_ref, f32[512,2048]{1,0:T(8,128)S(1)} %get-tuple-element.32.own_ref, ...), custom_call_target="tpu_custom_call", output_to_operand_aliasing={{}: (4, {})} | custom-call | tf_op jit(solution)/shard_map/place_b/pallas_call | solution.py:498
  107.9 1.9 %place_coef.1 = f32[3072,128]{1,0:T(8,128)} custom-call(s32[1]{0:T(128)} %bitcast.me_ref, s32[24]{0:T(128)S(1)} %get-tuple-element.33.table_ref, f32[512,128]{1,0:T(8,128)S(1)} %collective-permute-done.12.near_ref, f32[2048,128]{1,0:T(8,128)S(1)} %get-tuple-element.45.own_ref, f32[512,128]{1,0:T(8,128)S(1)} %collective-permute-done.13.far_ref), custom_call_target="tpu_custom_call" | custom-call | tf_op jit(solution)/shard_map/place_coef/pallas_call | solution.py:532
  (60 shorter events, 20.1 us)
Async XLA Ops:
  4.9 1.4 %collective-permute-start.2 = (f32[256,128]{1,0:T(8,128)S(1)}, f32[256,128]{1,0:T(8,128)S(1)}, u32[]{:S(2)}, u32[]{:S(2)}) collective-permute-start(f32[256,128]{1,0:T(8,128)S(1)} %get-tuple-element.39), channel_id=1, source_target_pairs={{0,1},{1,0},{2,3},{3,2},{4,5},{5,4},{6,7},{7,6},{8,9},{9,8},{10,11... | collective-permute-start | bytes 393224 | tf_op jit(solution)/shard_map/ppermute | solution.py:19
  6.4 7.1 %collective-permute-start.3 = (f32[256,128]{1,0:T(8,128)S(1)}, f32[256,128]{1,0:T(8,128)S(1)}, u32[]{:S(2)}, u32[]{:S(2)}) collective-permute-start(f32[256,128]{1,0:T(8,128)S(1)} %add.51), channel_id=1, source_target_pairs={{0,8},{1,5},{2,10},{3,7},{4,12},{5,1},{6,14},{7,3},{8,0},{9,13},{1... | collective-permute-start | bytes 393224 | tf_op jit(solution)/shard_map/ppermute | solution.py:447
  13.5 5.2 %collective-permute-start.4 = (f32[256,128]{1,0:T(8,128)S(1)}, f32[256,128]{1,0:T(8,128)S(1)}, u32[]{:S(2)}, u32[]{:S(2)}) collective-permute-start(f32[256,128]{1,0:T(8,128)S(1)} %add.52), channel_id=1, source_target_pairs={{0,2},{1,9},{2,0},{3,11},{4,6},{5,13},{6,4},{7,15},{8,10},{9,1},{1... | collective-permute-start | bytes 393224 | tf_op jit(solution)/shard_map/ppermute | solution.py:447
  18.7 5.4 %collective-permute-start.5 = (f32[256,128]{1,0:T(8,128)S(1)}, f32[256,128]{1,0:T(8,128)S(1)}, u32[]{:S(2)}, u32[]{:S(2)}) collective-permute-start(f32[256,128]{1,0:T(8,128)S(1)} %add.53), channel_id=1, source_target_pairs={{0,4},{1,3},{2,6},{3,1},{4,0},{5,7},{6,2},{7,5},{8,12},{9,11},{10,... | collective-permute-start | bytes 393224 | tf_op jit(solution)/shard_map/ppermute | solution.py:447
  24.1 1.4 %collective-permute-start.6 = (f32[256,128]{1,0:T(8,128)S(1)}, f32[256,128]{1,0:T(8,128)S(1)}, u32[]{:S(2)}, u32[]{:S(2)}) collective-permute-start(f32[256,128]{1,0:T(8,128)S(1)} %add.54.own_ref), channel_id=1, source_target_pairs={{0,1},{1,0},{2,3},{3,2},{4,5},{5,4},{6,7},{7,6},{8,9},{9,8},{10,11... | collective-permute-start | bytes 393224 | tf_op jit(solution)/shard_map/ppermute | solution.py:19
  26.9 1.4 %collective-permute-start.7 = (f32[256,128]{1,0:T(8,128)S(1)}, f32[256,128]{1,0:T(8,128)S(1)}, u32[]{:S(2)}, u32[]{:S(2)}) collective-permute-start(f32[256,128]{1,0:T(8,128)S(1)} %get-tuple-element.43), channel_id=1, source_target_pairs={{0,1},{1,0},{2,3},{3,2},{4,5},{5,4},{6,7},{7,6},{8,9},{9,8},{10,11... | collective-permute-start | bytes 393224 | tf_op jit(solution)/shard_map/ppermute | solution.py:19
  28.3 6.2 %collective-permute-start.8 = (f32[256,128]{1,0:T(8,128)S(1)}, f32[256,128]{1,0:T(8,128)S(1)}, u32[]{:S(2)}, u32[]{:S(2)}) collective-permute-start(f32[256,128]{1,0:T(8,128)S(1)} %add.55), channel_id=1, source_target_pairs={{0,8},{1,5},{2,10},{3,7},{4,12},{5,1},{6,14},{7,3},{8,0},{9,13},{1... | collective-permute-start | bytes 393224 | tf_op jit(solution)/shard_map/ppermute | solution.py:447
  34.6 5.0 %collective-permute-start.9 = (f32[256,128]{1,0:T(8,128)S(1)}, f32[256,128]{1,0:T(8,128)S(1)}, u32[]{:S(2)}, u32[]{:S(2)}) collective-permute-start(f32[256,128]{1,0:T(8,128)S(1)} %add.56), channel_id=1, source_target_pairs={{0,2},{1,9},{2,0},{3,11},{4,6},{5,13},{6,4},{7,15},{8,10},{9,1},{1... | collective-permute-start | bytes 393224 | tf_op jit(solution)/shard_map/ppermute | solution.py:447
  39.6 5.9 %collective-permute-start.10 = (f32[256,128]{1,0:T(8,128)S(1)}, f32[256,128]{1,0:T(8,128)S(1)}, u32[]{:S(2)}, u32[]{:S(2)}) collective-permute-start(f32[256,128]{1,0:T(8,128)S(1)} %add.57), channel_id=1, source_target_pairs={{0,4},{1,3},{2,6},{3,1},{4,0},{5,7},{6,2},{7,5},{8,12},{9,11},{10,... | collective-permute-start | bytes 393224 | tf_op jit(solution)/shard_map/ppermute | solution.py:447
  45.5 1.4 %collective-permute-start.11 = (f32[256,128]{1,0:T(8,128)S(1)}, f32[256,128]{1,0:T(8,128)S(1)}, u32[]{:S(2)}, u32[]{:S(2)}) collective-permute-start(f32[256,128]{1,0:T(8,128)S(1)} %add.58.own_ref), channel_id=1, source_target_pairs={{0,1},{1,0},{2,3},{3,2},{4,5},{5,4},{6,7},{7,6},{8,9},{9,8},{10,11... | collective-permute-start | bytes 393224 | tf_op jit(solution)/shard_map/ppermute | solution.py:19
  48.4 1.4 %collective-permute-start.15 = (f32[256,128]{1,0:T(8,128)S(1)}, f32[256,128]{1,0:T(8,128)S(1)}, u32[]{:S(2)}, u32[]{:S(2)}) collective-permute-start(f32[256,128]{1,0:T(8,128)S(1)} %get-tuple-element.50), channel_id=1, source_target_pairs={{0,1},{1,0},{2,3},{3,2},{4,5},{5,4},{6,7},{7,6},{8,9},{9,8},{10,11... | collective-permute-start | bytes 393224 | tf_op jit(solution)/shard_map/ppermute | solution.py:19
  49.8 5.9 %collective-permute-start.16 = (f32[256,128]{1,0:T(8,128)S(1)}, f32[256,128]{1,0:T(8,128)S(1)}, u32[]{:S(2)}, u32[]{:S(2)}) collective-permute-start(f32[256,128]{1,0:T(8,128)S(1)} %add.59), channel_id=1, source_target_pairs={{0,8},{1,5},{2,10},{3,7},{4,12},{5,1},{6,14},{7,3},{8,0},{9,13},{1... | collective-permute-start | bytes 393224 | tf_op jit(solution)/shard_map/ppermute | solution.py:447
  55.8 5.0 %collective-permute-start.17 = (f32[256,128]{1,0:T(8,128)S(1)}, f32[256,128]{1,0:T(8,128)S(1)}, u32[]{:S(2)}, u32[]{:S(2)}) collective-permute-start(f32[256,128]{1,0:T(8,128)S(1)} %add.60), channel_id=1, source_target_pairs={{0,2},{1,9},{2,0},{3,11},{4,6},{5,13},{6,4},{7,15},{8,10},{9,1},{1... | collective-permute-start | bytes 393224 | tf_op jit(solution)/shard_map/ppermute | solution.py:447
  60.8 5.9 %collective-permute-start.18 = (f32[256,128]{1,0:T(8,128)S(1)}, f32[256,128]{1,0:T(8,128)S(1)}, u32[]{:S(2)}, u32[]{:S(2)}) collective-permute-start(f32[256,128]{1,0:T(8,128)S(1)} %add.61), channel_id=1, source_target_pairs={{0,4},{1,3},{2,6},{3,1},{4,0},{5,7},{6,2},{7,5},{8,12},{9,11},{10,... | collective-permute-start | bytes 393224 | tf_op jit(solution)/shard_map/ppermute | solution.py:447
  63.8 36.7 %collective-permute-start = (f32[520,512]{1,0:T(8,128)S(1)}, f32[520,512]{1,0:T(8,128)S(1)}, u32[]{:S(2)}, u32[]{:S(2)}) collective-permute-start(f32[520,512]{1,0:T(8,128)S(1)} %get-tuple-element.30), channel_id=1, source_target_pairs={{0,1},{1,0},{2,3},{3,2},{4,5},{5,4},{6,7},{7,6},{8,9},{9,8},{10,11... | collective-permute-start | bytes 3194888 | tf_op jit(solution)/shard_map/ppermute | solution.py:19
  66.7 6.2 %collective-permute-start.19 = (f32[256,128]{1,0:T(8,128)S(1)}, f32[256,128]{1,0:T(8,128)S(1)}, u32[]{:S(2)}, u32[]{:S(2)}) collective-permute-start(f32[256,128]{1,0:T(8,128)S(1)} %add.62.own_ref), channel_id=1, source_target_pairs={{0,1},{1,0},{2,3},{3,2},{4,5},{5,4},{6,7},{7,6},{8,9},{9,8},{10,11... | collective-permute-start | bytes 393224 | tf_op jit(solution)/shard_map/ppermute | solution.py:19
  66.8 39.3 %collective-permute-start.14 = (f32[256,512]{1,0:T(8,128)S(1)}, f32[256,512]{1,0:T(8,128)S(1)}, u32[]{:S(2)}, u32[]{:S(2)}) collective-permute-start(f32[256,512]{1,0:T(8,128)S(1)} %get-tuple-element.47), channel_id=1, source_target_pairs={{0,15},{1,2},{2,1},{3,4},{4,3},{5,6},{6,5},{7,8},{8,7},{9,10},{10,... | collective-permute-start | bytes 1572872 | tf_op jit(solution)/shard_map/ppermute | solution.py:429
  72.2 28.2 %collective-permute-start.1 = (f32[264,512]{1,0:T(8,128)S(1)}, f32[264,512]{1,0:T(8,128)S(1)}, u32[]{:S(2)}, u32[]{:S(2)}) collective-permute-start(f32[264,512]{1,0:T(8,128)S(1)} %get-tuple-element.31), channel_id=1, source_target_pairs={{0,15},{1,2},{2,1},{3,4},{4,3},{5,6},{6,5},{7,8},{8,7},{9,10},{10,... | collective-permute-start | bytes 1622024 | tf_op jit(solution)/shard_map/ppermute | solution.py:429
  73.6 1.2 %collective-permute-start.20 = (f32[16,128]{1,0:T(8,128)S(1)}, f32[16,128]{1,0:T(8,128)S(1)}, u32[]{:S(2)}, u32[]{:S(2)}) collective-permute-start(f32[16,128]{1,0:T(8,128)S(1)} %get-tuple-element.53), channel_id=1, source_target_pairs={{0,1},{1,0},{2,3},{3,2},{4,5},{5,4},{6,7},{7,6},{8,9},{9,8},{10,11... | collective-permute-start | bytes 24584 | tf_op jit(solution)/shard_map/ppermute | solution.py:19
  74.9 18.5 %collective-permute-start.21 = (f32[16,128]{1,0:T(8,128)S(1)}, f32[16,128]{1,0:T(8,128)S(1)}, u32[]{:S(2)}, u32[]{:S(2)}) collective-permute-start(f32[16,128]{1,0:T(8,128)S(1)} %add_select_fusion.3), channel_id=1, source_target_pairs={{0,2},{1,3},{2,0},{3,1},{4,6},{5,7},{6,4},{7,5},{8,10},{9,11},{10,... | collective-permute-start | bytes 24584 | tf_op jit(solution)/shard_map/ppermute | solution.py:19
  93.6 3.7 %collective-permute-start.22 = (f32[16,128]{1,0:T(8,128)S(1)}, f32[16,128]{1,0:T(8,128)S(1)}, u32[]{:S(2)}, u32[]{:S(2)}) collective-permute-start(f32[16,128]{1,0:T(8,128)S(1)} %add_select_fusion.2), channel_id=1, source_target_pairs={{0,4},{1,5},{2,6},{3,7},{4,0},{5,1},{6,2},{7,3},{8,12},{9,13},{10,... | collective-permute-start | bytes 24584 | tf_op jit(solution)/shard_map/ppermute | solution.py:19
  95.6 12.3 %collective-permute-start.12 = (f32[512,128]{1,0:T(8,128)S(1)}, f32[512,128]{1,0:T(8,128)S(1)}, u32[]{:S(2)}, u32[]{:S(2)}) collective-permute-start(f32[512,128]{1,0:T(8,128)S(1)} %get-tuple-element.44), channel_id=1, source_target_pairs={{0,1},{1,0},{2,3},{3,2},{4,5},{5,4},{6,7},{7,6},{8,9},{9,8},{10,11... | collective-permute-start | bytes 786440 | tf_op jit(solution)/shard_map/ppermute | solution.py:19
  97.2 10.7 %collective-permute-start.13 = (f32[512,128]{1,0:T(8,128)S(1)}, f32[512,128]{1,0:T(8,128)S(1)}, u32[]{:S(2)}, u32[]{:S(2)}) collective-permute-start(f32[512,128]{1,0:T(8,128)S(1)} %get-tuple-element.46), channel_id=1, source_target_pairs={{0,15},{1,2},{2,1},{3,4},{4,3},{5,6},{6,5},{7,8},{8,7},{9,10},{10,... | collective-permute-start | bytes 786440 | tf_op jit(solution)/shard_map/ppermute | solution.py:429
  100.5 9.3 %collective-permute-start.23 = (f32[16,128]{1,0:T(8,128)S(1)}, f32[16,128]{1,0:T(8,128)S(1)}, u32[]{:S(2)}, u32[]{:S(2)}) collective-permute-start(f32[16,128]{1,0:T(8,128)S(1)} %add_select_fusion.1), channel_id=1, source_target_pairs={{0,8},{1,9},{2,10},{3,11},{4,12},{5,13},{6,14},{7,15},{8,0},{9,1},... | collective-permute-start | bytes 24584 | tf_op jit(solution)/shard_map/ppermute | solution.py:19
  (2 other events, 38.8 us)

commit v3 on v2

--- a/solution.py
+++ b/solution.py
@@ -88,15 +88,13 @@
 
 
 def first_kernel(
-    push, shards, chunk, me_ref, drop_ref, dest_ref, design_ref, now_ref, prev_ref,
-    send_ref, split_ref, near_ref, far_a_ref, far_b_ref, held_ref, high_ref, low_ref, base_ref, point_ref,
+    push, chunk, me_ref, design_ref, now_ref, prev_ref,
+    send_ref, split_ref, held_ref, high_ref, low_ref, base_ref, point_ref,
     prev, sems,
 ):
     me = me_ref[0]
     parity = me & 1
-    rows, feats = design_ref.shape
-    blocks = drop_ref.shape[0]
-    edge = chunk // LANE
+    _, feats = design_ref.shape
     steps = feats // chunk
     across = rows_of(1 - parity, send_ref.shape[0])
 
@@ -127,6 +125,15 @@
             send_ref[...] = ahead
         else:
             send_ref[...] += ahead
+
+
+def edges_kernel(shards, me_ref, drop_ref, dest_ref, held_ref, near_ref, far_a_ref, far_b_ref):
+    me = me_ref[0]
+    parity = me & 1
+    rows, feats = held_ref.shape
+    chunk = near_ref.shape[1]
+    edge = chunk // LANE
+    blocks = drop_ref.shape[0]
 
     def put(right, near):
         block = held_ref[:, feats - chunk :] if right else held_ref[:, :chunk]
@@ -405,12 +412,12 @@
         return jax.ShapeDtypeStruct(shape, jnp.bfloat16)
 
     drop, dest = in_hbm(drop_mask), in_hbm(dest_shard)
-    send, split, near, far_a, far_b, held, high, low, base, point = pl.pallas_call(
-        functools.partial(first_kernel, first_push, shards, chunk),
-        in_specs=[scalars()] * 3 + [anywhere] * 3,
-        out_specs=[whole()] * 10,
+    send, split, held, high, low, base, point = pl.pallas_call(
+        functools.partial(first_kernel, first_push, chunk),
+        in_specs=[scalars()] + [anywhere] * 3,
+        out_specs=[whole()] * 7,
         out_shape=[
-            f32(half, width), b16(feats, 2 * width), f32(samples + 8, chunk), f32(half + 8, chunk), f32(half, chunk),
+            f32(half, width), b16(feats, 2 * width),
             f32(samples, feats), b16(samples, feats), b16(samples, feats), f32(feats, width), f32(feats, width),
         ],
         scratch_shapes=[
@@ -419,7 +426,15 @@
         ],
         compiler_params=params,
         name="first",
-    )(me, drop, dest, in_hbm(design), in_hbm(coef_now), in_hbm(coef_prev))
+    )(me, in_hbm(design), in_hbm(coef_now), in_hbm(coef_prev))
+    near, far_a, far_b = pl.pallas_call(
+        functools.partial(edges_kernel, shards),
+        in_specs=[scalars()] * 3 + [whole()],
+        out_specs=[whole()] * 3,
+        out_shape=[f32(samples + 8, chunk), f32(half + 8, chunk), f32(half, chunk)],
+        compiler_params=params,
+        name="edges",
+    )(me, drop, dest, held)
 
     def inward(value):
         return swap(value, 1)

time: 111 us -> 110 us (level)
    pallas_call x1 -> x2, Pallas kernels: 4.25 us -> 4.25 us  [the longest x1 3.43 us: body(): pl.pallas_call(functools.partial(first_kernel, first_push, chunk), in_spe...]
where the time goes in v3:
time: 110 us
  waiting for transfers between devices  50.6 us (46%)
  starting transfers between devices  36 us (33%)
  Pallas kernels  21 us (19%)
    ppermute x9, waiting for transfers between devices, combine(): total = total + lax.ppermute(total, AXIS, pairs)  26.7 us
    ppermute x9, starting transfers between devices, combine(): total = total + lax.ppermute(total, AXIS, pairs)  24.1 us
    ppermute x12, waiting for transfers between devices, swap(): return lax.ppermute(value, AXIS, [(i, i ^ bit) for i in range(count)])  23.9 us
    ppermute x3, starting transfers between devices, outward(): return lax.ppermute(value, AXIS, pairs)  8.65 us
    pallas_call x1, Pallas kernels, body(): pl.pallas_call(functools.partial(first_kernel, first_push, chunk), in_spe...  3.43 us
    ppermute x12, starting transfers between devices, swap(): return lax.ppermute(value, AXIS, [(i, i ^ bit) for i in range(count)])  3.28 us
    pallas_call x1, Pallas kernels, body(): pl.pallas_call(place_a_kernel, in_specs=[scalars()] * 3 + [whole()] * 3,...  3.15 us
    pallas_call x2, Pallas kernels, descend(): pl.pallas_call(functools.partial(descend_kernel, ahead, chunk, lipschitz,...  2.82 us
  transfers between devices with their start and end apart: 24, of which 17 were waited for; matrix products, arithmetic and copies ran while one was open for 0% of the time, Pallas kernels for 13%

profile of v3, /device:TPU:0, one launch (start us, length us, event | category | flops | bytes accessed | tf_op | source)
XLA Modules:
  0.0 109.6 jit_solution(11098556410986778490)
XLA Ops:
  0.6 3.4 %first.1 = (f32[256,128]{1,0:T(8,128)S(1)}, bf16[2048,256]{1,0:T(8,128)(2,1)S(1)}, f32[512,2048]{1,0:T(8,128)S(1)}, bf16[512,2048]{1,0:T(8,128)(2,1)S(1)}, bf16[...) custom-call(s32[1]{0:T(128)} %bitcast.me_ref, f32[512,2048]{1,0:T(8,128)} %design_ref.1, ...), custom_call_target="tpu_custom_call" | custom-call | tf_op jit(solution)/shard_map/first/pallas_call | solution.py:415
  5.6 4.1 %collective-permute-start.3 = (f32[256,128]{1,0:T(8,128)S(1)}, f32[256,128]{1,0:T(8,128)S(1)}, u32[]{:S(2)}, u32[]{:S(2)}) collective-permute-start(f32[256,128]{1,0:T(8,128)S(1)} %add.51), channel_id=1, source_target_pairs={{0,8},{1,5},{2,10},{3,7},{4,12},{5,1},{6,14},{7,3},{8,0},{9,13},{1... | collective-permute-start | bytes 393224 | tf_op jit(solution)/shard_map/ppermute | solution.py:462
  9.7 3.0 %collective-permute-done.3 = f32[256,128]{1,0:T(8,128)S(1)} collective-permute-done((f32[256,128]{1,0:T(8,128)S(1)}, f32[256,128]{1,0:T(8,128)S(1)}, u32[]{:S(2)}, u32[]{:S(2)}) %collective-permute-start.3) | collective-permute-done | bytes 131104 | tf_op jit(solution)/shard_map/ppermute | solution.py:462
  12.7 2.2 %collective-permute-start.4 = (f32[256,128]{1,0:T(8,128)S(1)}, f32[256,128]{1,0:T(8,128)S(1)}, u32[]{:S(2)}, u32[]{:S(2)}) collective-permute-start(f32[256,128]{1,0:T(8,128)S(1)} %add.52), channel_id=1, source_target_pairs={{0,2},{1,9},{2,0},{3,11},{4,6},{5,13},{6,4},{7,15},{8,10},{9,1},{1... | collective-permute-start | bytes 393224 | tf_op jit(solution)/shard_map/ppermute | solution.py:462
  14.9 2.9 %collective-permute-done.4 = f32[256,128]{1,0:T(8,128)S(1)} collective-permute-done((f32[256,128]{1,0:T(8,128)S(1)}, f32[256,128]{1,0:T(8,128)S(1)}, u32[]{:S(2)}, u32[]{:S(2)}) %collective-permute-start.4) | collective-permute-done | bytes 131104 | tf_op jit(solution)/shard_map/ppermute | solution.py:462
  17.9 2.5 %collective-permute-start.5 = (f32[256,128]{1,0:T(8,128)S(1)}, f32[256,128]{1,0:T(8,128)S(1)}, u32[]{:S(2)}, u32[]{:S(2)}) collective-permute-start(f32[256,128]{1,0:T(8,128)S(1)} %add.53), channel_id=1, source_target_pairs={{0,4},{1,3},{2,6},{3,1},{4,0},{5,7},{6,2},{7,5},{8,12},{9,11},{10,... | collective-permute-start | bytes 393224 | tf_op jit(solution)/shard_map/ppermute | solution.py:462
  20.3 2.9 %collective-permute-done.5 = f32[256,128]{1,0:T(8,128)S(1)} collective-permute-done((f32[256,128]{1,0:T(8,128)S(1)}, f32[256,128]{1,0:T(8,128)S(1)}, u32[]{:S(2)}, u32[]{:S(2)}) %collective-permute-start.5) | collective-permute-done | bytes 131104 | tf_op jit(solution)/shard_map/ppermute | solution.py:462
  27.5 3.2 %collective-permute-start.8 = (f32[256,128]{1,0:T(8,128)S(1)}, f32[256,128]{1,0:T(8,128)S(1)}, u32[]{:S(2)}, u32[]{:S(2)}) collective-permute-start(f32[256,128]{1,0:T(8,128)S(1)} %add.55), channel_id=1, source_target_pairs={{0,8},{1,5},{2,10},{3,7},{4,12},{5,1},{6,14},{7,3},{8,0},{9,13},{1... | collective-permute-start | bytes 393224 | tf_op jit(solution)/shard_map/ppermute | solution.py:462
  30.8 2.9 %collective-permute-done.8 = f32[256,128]{1,0:T(8,128)S(1)} collective-permute-done((f32[256,128]{1,0:T(8,128)S(1)}, f32[256,128]{1,0:T(8,128)S(1)}, u32[]{:S(2)}, u32[]{:S(2)}) %collective-permute-start.8) | collective-permute-done | bytes 131104 | tf_op jit(solution)/shard_map/ppermute | solution.py:462
  35.3 3.4 %collective-permute-done.9 = f32[256,128]{1,0:T(8,128)S(1)} collective-permute-done((f32[256,128]{1,0:T(8,128)S(1)}, f32[256,128]{1,0:T(8,128)S(1)}, u32[]{:S(2)}, u32[]{:S(2)}) %collective-permute-start.9) | collective-permute-done | bytes 131104 | tf_op jit(solution)/shard_map/ppermute | solution.py:462
  38.8 2.9 %collective-permute-start.10 = (f32[256,128]{1,0:T(8,128)S(1)}, f32[256,128]{1,0:T(8,128)S(1)}, u32[]{:S(2)}, u32[]{:S(2)}) collective-permute-start(f32[256,128]{1,0:T(8,128)S(1)} %add.57), channel_id=1, source_target_pairs={{0,4},{1,3},{2,6},{3,1},{4,0},{5,7},{6,2},{7,5},{8,12},{9,11},{10,... | collective-permute-start | bytes 393224 | tf_op jit(solution)/shard_map/ppermute | solution.py:462
  41.7 2.9 %collective-permute-done.10 = f32[256,128]{1,0:T(8,128)S(1)} collective-permute-done((f32[256,128]{1,0:T(8,128)S(1)}, f32[256,128]{1,0:T(8,128)S(1)}, u32[]{:S(2)}, u32[]{:S(2)}) %collective-permute-start.10) | collective-permute-done | bytes 131104 | tf_op jit(solution)/shard_map/ppermute | solution.py:462
  49.0 3.0 %collective-permute-start.16 = (f32[256,128]{1,0:T(8,128)S(1)}, f32[256,128]{1,0:T(8,128)S(1)}, u32[]{:S(2)}, u32[]{:S(2)}) collective-permute-start(f32[256,128]{1,0:T(8,128)S(1)} %add.59), channel_id=1, source_target_pairs={{0,8},{1,5},{2,10},{3,7},{4,12},{5,1},{6,14},{7,3},{8,0},{9,13},{1... | collective-permute-start | bytes 393224 | tf_op jit(solution)/shard_map/ppermute | solution.py:462
  52.0 3.0 %collective-permute-done.16 = f32[256,128]{1,0:T(8,128)S(1)} collective-permute-done((f32[256,128]{1,0:T(8,128)S(1)}, f32[256,128]{1,0:T(8,128)S(1)}, u32[]{:S(2)}, u32[]{:S(2)}) %collective-permute-start.16) | collective-permute-done | bytes 131104 | tf_op jit(solution)/shard_map/ppermute | solution.py:462
  56.6 3.4 %collective-permute-done.17 = f32[256,128]{1,0:T(8,128)S(1)} collective-permute-done((f32[256,128]{1,0:T(8,128)S(1)}, f32[256,128]{1,0:T(8,128)S(1)}, u32[]{:S(2)}, u32[]{:S(2)}) %collective-permute-start.17) | collective-permute-done | bytes 131104 | tf_op jit(solution)/shard_map/ppermute | solution.py:462
  60.0 2.9 %collective-permute-start.18 = (f32[256,128]{1,0:T(8,128)S(1)}, f32[256,128]{1,0:T(8,128)S(1)}, u32[]{:S(2)}, u32[]{:S(2)}) collective-permute-start(f32[256,128]{1,0:T(8,128)S(1)} %add.61), channel_id=1, source_target_pairs={{0,4},{1,3},{2,6},{3,1},{4,0},{5,7},{6,2},{7,5},{8,12},{9,11},{10,... | collective-permute-start | bytes 393224 | tf_op jit(solution)/shard_map/ppermute | solution.py:462
  63.9 2.0 %collective-permute-done.18 = f32[256,128]{1,0:T(8,128)S(1)} collective-permute-done((f32[256,128]{1,0:T(8,128)S(1)}, f32[256,128]{1,0:T(8,128)S(1)}, u32[]{:S(2)}, u32[]{:S(2)}) %collective-permute-start.18) | collective-permute-done | bytes 131104 | tf_op jit(solution)/shard_map/ppermute | solution.py:462
  66.0 5.4 %collective-permute-start.14 = (f32[256,512]{1,0:T(8,128)S(1)}, f32[256,512]{1,0:T(8,128)S(1)}, u32[]{:S(2)}, u32[]{:S(2)}) collective-permute-start(f32[256,512]{1,0:T(8,128)S(1)} %get-tuple-element.47), channel_id=1, source_target_pairs={{0,15},{1,2},{2,1},{3,4},{4,3},{5,6},{6,5},{7,8},{8,7},{9,10},{10,... | collective-permute-start | bytes 1572872 | tf_op jit(solution)/shard_map/ppermute | solution.py:444
  74.1 18.5 %collective-permute-done.21 = f32[16,128]{1,0:T(8,128)S(1)} collective-permute-done((f32[16,128]{1,0:T(8,128)S(1)}, f32[16,128]{1,0:T(8,128)S(1)}, u32[]{:S(2)}, u32[]{:S(2)}) %collective-permute-start.21) | collective-permute-done | bytes 8224 | tf_op jit(solution)/shard_map/ppermute | solution.py:19
  92.7 2.0 %collective-permute-start.22 = (f32[16,128]{1,0:T(8,128)S(1)}, f32[16,128]{1,0:T(8,128)S(1)}, u32[]{:S(2)}, u32[]{:S(2)}) collective-permute-start(f32[16,128]{1,0:T(8,128)S(1)} %add_select_fusion.2), channel_id=1, source_target_pairs={{0,4},{1,5},{2,6},{3,7},{4,0},{5,1},{6,2},{7,3},{8,12},{9,13},{10,... | collective-permute-start | bytes 24584 | tf_op jit(solution)/shard_map/ppermute | solution.py:19
  96.4 3.2 %collective-permute-start.13 = (f32[512,128]{1,0:T(8,128)S(1)}, f32[512,128]{1,0:T(8,128)S(1)}, u32[]{:S(2)}, u32[]{:S(2)}) collective-permute-start(f32[512,128]{1,0:T(8,128)S(1)} %get-tuple-element.46), channel_id=1, source_target_pairs={{0,15},{1,2},{2,1},{3,4},{4,3},{5,6},{6,5},{7,8},{8,7},{9,10},{10,... | collective-permute-start | bytes 786440 | tf_op jit(solution)/shard_map/ppermute | solution.py:444
  99.7 3.1 %place_a.1 = (f32[512,3072]{1,0:T(8,128)}, s32[24]{0:T(128)S(1)}) custom-call(s32[1]{0:T(128)} %bitcast.me_ref, s32[16]{0:T(128)} %drop_ref.3, s32[16]{0:T(128)} %dest_ref.3, f32[520,512]{1,0:T(8,128)S(1)} %collective-permute-done.near_ref, f32[264,512]{1,0:T(8,128)S(1)} %collective-permute-done.1.far_ref.far_a_ref, ...), custom_call_target="tpu_custom_call" | custom-call | tf_op jit(solution)/shard_map/place_a/pallas_call | solution.py:504
  102.8 2.4 %place_b.1.given_ref = f32[512,3072]{1,0:T(8,128)} custom-call(s32[1]{0:T(128)} %bitcast.me_ref, s32[24]{0:T(128)S(1)} %get-tuple-element.33.table_ref, f32[520,512]{1,0:T(8,128)S(1)} %collective-permute-done.near_ref, f32[512,2048]{1,0:T(8,128)S(1)} %get-tuple-element.30.held_ref.own_ref, ...), custom_call_target="tpu_custom_call", output_to_operand_aliasing={{}: (4, {})} | custom-call | tf_op jit(solution)/shard_map/place_b/pallas_call | solution.py:513
  107.1 1.9 %place_coef.1 = f32[3072,128]{1,0:T(8,128)} custom-call(s32[1]{0:T(128)} %bitcast.me_ref, s32[24]{0:T(128)S(1)} %get-tuple-element.33.table_ref, f32[512,128]{1,0:T(8,128)S(1)} %collective-permute-done.12.near_ref, f32[2048,128]{1,0:T(8,128)S(1)} %get-tuple-element.45.own_ref, f32[512,128]{1,0:T(8,128)S(1)} %collective-permute-done.13.far_ref), custom_call_target="tpu_custom_call" | custom-call | tf_op jit(solution)/shard_map/place_coef/pallas_call | solution.py:547
  (61 shorter events, 21.1 us)
Async XLA Ops:
  4.1 1.5 %collective-permute-start.2 = (f32[256,128]{1,0:T(8,128)S(1)}, f32[256,128]{1,0:T(8,128)S(1)}, u32[]{:S(2)}, u32[]{:S(2)}) collective-permute-start(f32[256,128]{1,0:T(8,128)S(1)} %get-tuple-element.39), channel_id=1, source_target_pairs={{0,1},{1,0},{2,3},{3,2},{4,5},{5,4},{6,7},{7,6},{8,9},{9,8},{10,11... | collective-permute-start | bytes 393224 | tf_op jit(solution)/shard_map/ppermute | solution.py:19
  5.6 7.1 %collective-permute-start.3 = (f32[256,128]{1,0:T(8,128)S(1)}, f32[256,128]{1,0:T(8,128)S(1)}, u32[]{:S(2)}, u32[]{:S(2)}) collective-permute-start(f32[256,128]{1,0:T(8,128)S(1)} %add.51), channel_id=1, source_target_pairs={{0,8},{1,5},{2,10},{3,7},{4,12},{5,1},{6,14},{7,3},{8,0},{9,13},{1... | collective-permute-start | bytes 393224 | tf_op jit(solution)/shard_map/ppermute | solution.py:462
  12.7 5.2 %collective-permute-start.4 = (f32[256,128]{1,0:T(8,128)S(1)}, f32[256,128]{1,0:T(8,128)S(1)}, u32[]{:S(2)}, u32[]{:S(2)}) collective-permute-start(f32[256,128]{1,0:T(8,128)S(1)} %add.52), channel_id=1, source_target_pairs={{0,2},{1,9},{2,0},{3,11},{4,6},{5,13},{6,4},{7,15},{8,10},{9,1},{1... | collective-permute-start | bytes 393224 | tf_op jit(solution)/shard_map/ppermute | solution.py:462
  17.9 5.4 %collective-permute-start.5 = (f32[256,128]{1,0:T(8,128)S(1)}, f32[256,128]{1,0:T(8,128)S(1)}, u32[]{:S(2)}, u32[]{:S(2)}) collective-permute-start(f32[256,128]{1,0:T(8,128)S(1)} %add.53), channel_id=1, source_target_pairs={{0,4},{1,3},{2,6},{3,1},{4,0},{5,7},{6,2},{7,5},{8,12},{9,11},{10,... | collective-permute-start | bytes 393224 | tf_op jit(solution)/shard_map/ppermute | solution.py:462
  23.3 1.4 %collective-permute-start.6 = (f32[256,128]{1,0:T(8,128)S(1)}, f32[256,128]{1,0:T(8,128)S(1)}, u32[]{:S(2)}, u32[]{:S(2)}) collective-permute-start(f32[256,128]{1,0:T(8,128)S(1)} %add.54.own_ref), channel_id=1, source_target_pairs={{0,1},{1,0},{2,3},{3,2},{4,5},{5,4},{6,7},{7,6},{8,9},{9,8},{10,11... | collective-permute-start | bytes 393224 | tf_op jit(solution)/shard_map/ppermute | solution.py:19
  26.1 1.4 %collective-permute-start.7 = (f32[256,128]{1,0:T(8,128)S(1)}, f32[256,128]{1,0:T(8,128)S(1)}, u32[]{:S(2)}, u32[]{:S(2)}) collective-permute-start(f32[256,128]{1,0:T(8,128)S(1)} %get-tuple-element.43), channel_id=1, source_target_pairs={{0,1},{1,0},{2,3},{3,2},{4,5},{5,4},{6,7},{7,6},{8,9},{9,8},{10,11... | collective-permute-start | bytes 393224 | tf_op jit(solution)/shard_map/ppermute | solution.py:19
  27.5 6.2 %collective-permute-start.8 = (f32[256,128]{1,0:T(8,128)S(1)}, f32[256,128]{1,0:T(8,128)S(1)}, u32[]{:S(2)}, u32[]{:S(2)}) collective-permute-start(f32[256,128]{1,0:T(8,128)S(1)} %add.55), channel_id=1, source_target_pairs={{0,8},{1,5},{2,10},{3,7},{4,12},{5,1},{6,14},{7,3},{8,0},{9,13},{1... | collective-permute-start | bytes 393224 | tf_op jit(solution)/shard_map/ppermute | solution.py:462
  33.7 5.0 %collective-permute-start.9 = (f32[256,128]{1,0:T(8,128)S(1)}, f32[256,128]{1,0:T(8,128)S(1)}, u32[]{:S(2)}, u32[]{:S(2)}) collective-permute-start(f32[256,128]{1,0:T(8,128)S(1)} %add.56), channel_id=1, source_target_pairs={{0,2},{1,9},{2,0},{3,11},{4,6},{5,13},{6,4},{7,15},{8,10},{9,1},{1... | collective-permute-start | bytes 393224 | tf_op jit(solution)/shard_map/ppermute | solution.py:462
  38.8 5.9 %collective-permute-start.10 = (f32[256,128]{1,0:T(8,128)S(1)}, f32[256,128]{1,0:T(8,128)S(1)}, u32[]{:S(2)}, u32[]{:S(2)}) collective-permute-start(f32[256,128]{1,0:T(8,128)S(1)} %add.57), channel_id=1, source_target_pairs={{0,4},{1,3},{2,6},{3,1},{4,0},{5,7},{6,2},{7,5},{8,12},{9,11},{10,... | collective-permute-start | bytes 393224 | tf_op jit(solution)/shard_map/ppermute | solution.py:462
  44.7 1.4 %collective-permute-start.11 = (f32[256,128]{1,0:T(8,128)S(1)}, f32[256,128]{1,0:T(8,128)S(1)}, u32[]{:S(2)}, u32[]{:S(2)}) collective-permute-start(f32[256,128]{1,0:T(8,128)S(1)} %add.58.own_ref), channel_id=1, source_target_pairs={{0,1},{1,0},{2,3},{3,2},{4,5},{5,4},{6,7},{7,6},{8,9},{9,8},{10,11... | collective-permute-start | bytes 393224 | tf_op jit(solution)/shard_map/ppermute | solution.py:19
  47.6 1.4 %collective-permute-start.15 = (f32[256,128]{1,0:T(8,128)S(1)}, f32[256,128]{1,0:T(8,128)S(1)}, u32[]{:S(2)}, u32[]{:S(2)}) collective-permute-start(f32[256,128]{1,0:T(8,128)S(1)} %get-tuple-element.50), channel_id=1, source_target_pairs={{0,1},{1,0},{2,3},{3,2},{4,5},{5,4},{6,7},{7,6},{8,9},{9,8},{10,11... | collective-permute-start | bytes 393224 | tf_op jit(solution)/shard_map/ppermute | solution.py:19
  49.0 5.9 %collective-permute-start.16 = (f32[256,128]{1,0:T(8,128)S(1)}, f32[256,128]{1,0:T(8,128)S(1)}, u32[]{:S(2)}, u32[]{:S(2)}) collective-permute-start(f32[256,128]{1,0:T(8,128)S(1)} %add.59), channel_id=1, source_target_pairs={{0,8},{1,5},{2,10},{3,7},{4,12},{5,1},{6,14},{7,3},{8,0},{9,13},{1... | collective-permute-start | bytes 393224 | tf_op jit(solution)/shard_map/ppermute | solution.py:462
  55.0 5.0 %collective-permute-start.17 = (f32[256,128]{1,0:T(8,128)S(1)}, f32[256,128]{1,0:T(8,128)S(1)}, u32[]{:S(2)}, u32[]{:S(2)}) collective-permute-start(f32[256,128]{1,0:T(8,128)S(1)} %add.60), channel_id=1, source_target_pairs={{0,2},{1,9},{2,0},{3,11},{4,6},{5,13},{6,4},{7,15},{8,10},{9,1},{1... | collective-permute-start | bytes 393224 | tf_op jit(solution)/shard_map/ppermute | solution.py:462
  60.0 5.9 %collective-permute-start.18 = (f32[256,128]{1,0:T(8,128)S(1)}, f32[256,128]{1,0:T(8,128)S(1)}, u32[]{:S(2)}, u32[]{:S(2)}) collective-permute-start(f32[256,128]{1,0:T(8,128)S(1)} %add.61), channel_id=1, source_target_pairs={{0,4},{1,3},{2,6},{3,1},{4,0},{5,7},{6,2},{7,5},{8,12},{9,11},{10,... | collective-permute-start | bytes 393224 | tf_op jit(solution)/shard_map/ppermute | solution.py:462
  63.8 35.9 %collective-permute-start = (f32[520,512]{1,0:T(8,128)S(1)}, f32[520,512]{1,0:T(8,128)S(1)}, u32[]{:S(2)}, u32[]{:S(2)}) collective-permute-start(f32[520,512]{1,0:T(8,128)S(1)} %get-tuple-element.31), channel_id=1, source_target_pairs={{0,1},{1,0},{2,3},{3,2},{4,5},{5,4},{6,7},{7,6},{8,9},{9,8},{10,11... | collective-permute-start | bytes 3194888 | tf_op jit(solution)/shard_map/ppermute | solution.py:19
  65.9 6.2 %collective-permute-start.19 = (f32[256,128]{1,0:T(8,128)S(1)}, f32[256,128]{1,0:T(8,128)S(1)}, u32[]{:S(2)}, u32[]{:S(2)}) collective-permute-start(f32[256,128]{1,0:T(8,128)S(1)} %add.62.own_ref), channel_id=1, source_target_pairs={{0,1},{1,0},{2,3},{3,2},{4,5},{5,4},{6,7},{7,6},{8,9},{9,8},{10,11... | collective-permute-start | bytes 393224 | tf_op jit(solution)/shard_map/ppermute | solution.py:19
  66.0 39.3 %collective-permute-start.14 = (f32[256,512]{1,0:T(8,128)S(1)}, f32[256,512]{1,0:T(8,128)S(1)}, u32[]{:S(2)}, u32[]{:S(2)}) collective-permute-start(f32[256,512]{1,0:T(8,128)S(1)} %get-tuple-element.47), channel_id=1, source_target_pairs={{0,15},{1,2},{2,1},{3,4},{4,3},{5,6},{6,5},{7,8},{8,7},{9,10},{10,... | collective-permute-start | bytes 1572872 | tf_op jit(solution)/shard_map/ppermute | solution.py:444
  71.4 28.2 %collective-permute-start.1 = (f32[264,512]{1,0:T(8,128)S(1)}, f32[264,512]{1,0:T(8,128)S(1)}, u32[]{:S(2)}, u32[]{:S(2)}) collective-permute-start(f32[264,512]{1,0:T(8,128)S(1)} %get-tuple-element.32), channel_id=1, source_target_pairs={{0,15},{1,2},{2,1},{3,4},{4,3},{5,6},{6,5},{7,8},{8,7},{9,10},{10,... | collective-permute-start | bytes 1622024 | tf_op jit(solution)/shard_map/ppermute | solution.py:444
  72.8 1.2 %collective-permute-start.20 = (f32[16,128]{1,0:T(8,128)S(1)}, f32[16,128]{1,0:T(8,128)S(1)}, u32[]{:S(2)}, u32[]{:S(2)}) collective-permute-start(f32[16,128]{1,0:T(8,128)S(1)} %get-tuple-element.53), channel_id=1, source_target_pairs={{0,1},{1,0},{2,3},{3,2},{4,5},{5,4},{6,7},{7,6},{8,9},{9,8},{10,11... | collective-permute-start | bytes 24584 | tf_op jit(solution)/shard_map/ppermute | solution.py:19
  74.1 18.5 %collective-permute-start.21 = (f32[16,128]{1,0:T(8,128)S(1)}, f32[16,128]{1,0:T(8,128)S(1)}, u32[]{:S(2)}, u32[]{:S(2)}) collective-permute-start(f32[16,128]{1,0:T(8,128)S(1)} %add_select_fusion.3), channel_id=1, source_target_pairs={{0,2},{1,3},{2,0},{3,1},{4,6},{5,7},{6,4},{7,5},{8,10},{9,11},{10,... | collective-permute-start | bytes 24584 | tf_op jit(solution)/shard_map/ppermute | solution.py:19
  92.7 3.7 %collective-permute-start.22 = (f32[16,128]{1,0:T(8,128)S(1)}, f32[16,128]{1,0:T(8,128)S(1)}, u32[]{:S(2)}, u32[]{:S(2)}) collective-permute-start(f32[16,128]{1,0:T(8,128)S(1)} %add_select_fusion.2), channel_id=1, source_target_pairs={{0,4},{1,5},{2,6},{3,7},{4,0},{5,1},{6,2},{7,3},{8,12},{9,13},{10,... | collective-permute-start | bytes 24584 | tf_op jit(solution)/shard_map/ppermute | solution.py:19
  94.8 12.3 %collective-permute-start.12 = (f32[512,128]{1,0:T(8,128)S(1)}, f32[512,128]{1,0:T(8,128)S(1)}, u32[]{:S(2)}, u32[]{:S(2)}) collective-permute-start(f32[512,128]{1,0:T(8,128)S(1)} %get-tuple-element.44), channel_id=1, source_target_pairs={{0,1},{1,0},{2,3},{3,2},{4,5},{5,4},{6,7},{7,6},{8,9},{9,8},{10,11... | collective-permute-start | bytes 786440 | tf_op jit(solution)/shard_map/ppermute | solution.py:19
  96.4 10.7 %collective-permute-start.13 = (f32[512,128]{1,0:T(8,128)S(1)}, f32[512,128]{1,0:T(8,128)S(1)}, u32[]{:S(2)}, u32[]{:S(2)}) collective-permute-start(f32[512,128]{1,0:T(8,128)S(1)} %get-tuple-element.46), channel_id=1, source_target_pairs={{0,15},{1,2},{2,1},{3,4},{4,3},{5,6},{6,5},{7,8},{8,7},{9,10},{10,... | collective-permute-start | bytes 786440 | tf_op jit(solution)/shard_map/ppermute | solution.py:444
  99.7 9.3 %collective-permute-start.23 = (f32[16,128]{1,0:T(8,128)S(1)}, f32[16,128]{1,0:T(8,128)S(1)}, u32[]{:S(2)}, u32[]{:S(2)}) collective-permute-start(f32[16,128]{1,0:T(8,128)S(1)} %add_select_fusion.1), channel_id=1, source_target_pairs={{0,8},{1,9},{2,10},{3,11},{4,12},{5,13},{6,14},{7,15},{8,0},{9,1},... | collective-permute-start | bytes 24584 | tf_op jit(solution)/shard_map/ppermute | solution.py:19
  (2 other events, 38.8 us)
